TPU v7x, 32 devices: a whole 2x2x4 slice. The times are simulated.
32 devices in a mesh: ctx: 8 (over z, y), tp: 4 (over x, core).
Axes of the slice: x: 2, y: 2, z: 4, core: 2. Of those that a mesh axis runs over, the one named last changes fastest.
Arguments:
- tokens: bfloat16 [2048, 5376], P('ctx', 'tp'), as said below
- out_grad: bfloat16 [2048, 5376], P('ctx', 'tp'), may hold values from -6 to 6
- in_gain: float32 [5376], replicated, may hold values from 0.5 to 1.5
- query_gain: float32 [128], replicated, may hold values from 0.25 to 1.75
- key_gain: float32 [128], replicated, may hold values from 0.25 to 1.75
- post_gain: float32 [5376], replicated, may hold values from 0.5 to 1.5
- q_codes: int32 [5376, 2048], P('ctx', 'tp'), may hold values from 0 to 15
- q_scodes: int32 [5376, 32], P('ctx', 'tp'), may hold values from 0 to 255
- q_second: float32 [21, 32], P(None, 'tp'), as said below
- kv_codes: int32 [2, 5376, 1024], P(None, 'ctx', 'tp'), may hold values from 0 to 15
- kv_scodes: int32 [2, 5376, 16], P(None, 'ctx', 'tp'), may hold values from 0 to 255
- kv_second: float32 [2, 21, 16], P(None, None, 'tp'), as said below
- o_codes: int32 [5376, 2048], P('ctx', 'tp'), may hold values from 0 to 15
- o_scodes: int32 [5376, 32], P('ctx', 'tp'), may hold values from 0 to 255
- o_second: float32 [21, 32], P(None, 'tp'), as said below
- q_down: bfloat16 [5376, 16], replicated, may hold values from -0.078125 to 0.078125
- query_up: bfloat16 [16, 2048], P(None, 'tp'), may hold values from -0.23925781 to 0.23925781
- kv_down: bfloat16 [2, 5376, 16], replicated, may hold values from -0.078125 to 0.078125
- key_value_up: bfloat16 [2, 16, 1024], P(None, None, 'tp'), may hold values from -0.23925781 to 0.23925781
- output_down: bfloat16 [2048, 16], P('tp'), may hold values from -0.125 to 0.125
- output_up: bfloat16 [16, 5376], replicated, may hold values from -0.23925781 to 0.23925781
Outputs:
- mixed: bfloat16 [2048, 5376], P('ctx', 'tp')
- tokens_grad: float32 [2048, 5376], P('ctx', 'tp')
- query_down_gradient: float32 [5376, 16], replicated
- query_up_gradient: float32 [16, 2048], P(None, 'tp')
- key_value_down_gradient: float32 [2, 5376, 16], replicated
- key_value_up_gradient: float32 [2, 16, 1024], P(None, None, 'tp')
- output_down_gradient: float32 [2048, 16], P('tp')
- output_up_gradient: float32 [16, 5376], replicated
- in_projection: float32 [2048, 1], P('ctx')
Inputs may be any that keep to these rules, and one draw needn't show every extreme that they name: `q_second`: positive, between one and eight over the square root of 5376. `kv_second`: positive, between one and eight over the square root of 5376. `o_second`: positive, between one and eight over the square root of 2048. `tokens`: real-valued activations of magnitude up to some tens.
All inputs are finite; a program needn't handle non-finite values.
Results may differ from a plain program's by a relative error of at most 0.015.
Values may be sent and summed in bfloat16 or wider, within the bound.
A program may use at most 128 MiB of HBM per device.

v0:
```python
import jax
import jax.numpy as jnp
from jax import lax
from jax.sharding import PartitionSpec as P

D = 5376
HEAD_SIZE = 128
WINDOW_TOKENS = 1024
QBLOCK = 64
QGROUP = 256


NORMAL_FLOAT = (
    -1.0,
    -0.6961928009986877,
    -0.5250730514526367,
    -0.39491748809814453,
    -0.28444138169288635,
    -0.18477343022823334,
    -0.09105003625154495,
    0.0,
    0.07958029955625534,
    0.16093020141124725,
    0.24611230194568634,
    0.33791524171829224,
    0.44070982933044434,
    0.5626170039176941,
    0.7229568362236023,
    1.0,
)
EPSILON = 1e-06
ADAPTER_SCALE = 2.0
SCORE_SCALE = 168.0 ** (-0.5)
ROPE_BASE = 10000.0


def from_behind(shard, axis, by):
    devices = lax.axis_size(axis)
    pairs = [(i, i + by) for i in range(devices) if 0 <= i + by < devices]
    return lax.ppermute(shard, axis, pairs)


def dequantize(codes, scodes, second, row_start):
    height, width = codes.shape
    levels = jnp.zeros(codes.shape, jnp.float32)
    for level in range(16):
        levels = jnp.where(codes == level, jnp.float32(NORMAL_FLOAT[level]), levels)
    group_ids = (row_start + jnp.arange(height, dtype=jnp.int32)) // QGROUP
    group_list = jnp.arange(second.shape[0], dtype=jnp.int32)
    picker = (group_ids[:, None] == group_list[None, :]).astype(jnp.float32)
    second_rows = jnp.dot(picker, second, precision=lax.Precision.HIGHEST)
    absmax = second_rows * ((scodes.astype(jnp.float32) + 1.0) / 256.0)
    scaled = levels.reshape(height, width // QBLOCK, QBLOCK) * absmax[:, :, None]
    return scaled.reshape(height, width).astype(jnp.bfloat16)


def rope_tables(positions):
    half = HEAD_SIZE // 2
    exponent = jnp.arange(half, dtype=jnp.float32) * (2.0 / HEAD_SIZE)
    frequency = jnp.power(jnp.float32(ROPE_BASE), -exponent)
    angle = positions.astype(jnp.float32)[:, None] * frequency[None, :]
    return (jnp.cos(angle), jnp.sin(angle))


def rotate(heads, cosine, sine):
    half = heads.shape[-1] // 2
    first = heads[..., :half]
    second = heads[..., half:]
    across = cosine[:, None, :]
    along = sine[:, None, :]
    return jnp.concatenate(
        [first * across - second * along, second * across + first * along], axis=-1
    )


def unrotate(grad, cosine, sine):
    half = grad.shape[-1] // 2
    first = grad[..., :half]
    second = grad[..., half:]
    across = cosine[:, None, :]
    along = sine[:, None, :]
    return jnp.concatenate(
        [first * across + second * along, second * across - first * along], axis=-1
    )


def head_norm(heads, gain):
    scale = lax.rsqrt(jnp.mean(heads * heads, axis=-1, keepdims=True) + EPSILON)
    return (heads * scale * gain, scale)


def head_norm_back(heads, scale, gain, grad):
    weighted = grad * gain
    inner = jnp.mean(weighted * heads, axis=-1, keepdims=True)
    return scale * weighted - scale**3 * heads * inner


def probabilities(q_rot, keys, query_pos, key_pos):
    count, q_heads, width = q_rot.shape
    kv_heads = keys.shape[1]
    grouped = q_rot.reshape(count, kv_heads, q_heads // kv_heads, width)
    scores = (
        jnp.einsum("tkgd,lkd->kgtl", grouped, keys, preferred_element_type=jnp.float32)
        * SCORE_SCALE
    )
    gap = query_pos[:, None] - key_pos[None, :]
    allowed = (gap >= 0) & (gap < WINDOW_TOKENS) & (key_pos[None, :] >= 0)
    weights = jnp.where(allowed, jnp.exp(scores), 0.0)
    return (weights / jnp.sum(weights, axis=-1, keepdims=True), grouped)


def attention_forward(q_rot, keys, values, query_pos, key_pos):
    count, q_heads, width = q_rot.shape
    probability, grouped = probabilities(q_rot, keys, query_pos, key_pos)
    prob_low = probability.astype(jnp.bfloat16)
    mixed = jnp.einsum("kgtl,lkd->tkgd", prob_low, values, preferred_element_type=jnp.float32)
    return mixed.reshape(count, q_heads * width).astype(jnp.bfloat16)


def attention_backward(q_rot, keys, values, output_gradient, query_pos, key_pos):
    count, q_heads, width = q_rot.shape
    kv_heads = keys.shape[1]
    probability, grouped = probabilities(q_rot, keys, query_pos, key_pos)
    prob_low = probability.astype(jnp.bfloat16)
    grad_grouped = output_gradient.reshape(count, kv_heads, q_heads // kv_heads, width)
    grad_prob = jnp.einsum(
        "tkgd,lkd->kgtl", grad_grouped, values, preferred_element_type=jnp.float32
    )
    grad_values = jnp.einsum(
        "kgtl,tkgd->lkd", prob_low, grad_grouped, preferred_element_type=jnp.float32
    )
    inner = jnp.sum(probability * grad_prob, axis=-1, keepdims=True)
    grad_scores = (probability * (grad_prob - inner) * SCORE_SCALE).astype(jnp.bfloat16)
    grad_query = jnp.einsum(
        "kgtl,lkd->tkgd", grad_scores, keys, preferred_element_type=jnp.float32
    ).reshape(count, q_heads, width)
    grad_keys = jnp.einsum(
        "kgtl,tkgd->lkd", grad_scores, grouped, preferred_element_type=jnp.float32
    )
    return (grad_query, grad_keys, grad_values)


def on_device(
    tokens,
    out_grad,
    in_gain,
    query_gain,
    key_gain,
    post_gain,
    q_codes,
    q_scodes,
    q_second,
    kv_codes,
    kv_scodes,
    kv_second,
    o_codes,
    o_scodes,
    o_second,
    q_down,
    query_up,
    kv_down,
    key_value_up,
    output_down,
    output_up,
):
    count = tokens.shape[0]
    share = tokens.shape[1]
    ctx_rank = lax.axis_index("ctx")
    tp_rank = lax.axis_index("tp")
    column_start = tp_rank * share
    row_start = ctx_rank * q_codes.shape[0]
    q_width = query_up.shape[1]
    kv_width = key_value_up.shape[2]
    q_heads_here = q_width // HEAD_SIZE
    kv_heads_here = kv_width // HEAD_SIZE
    q_part = dequantize(q_codes, q_scodes, q_second, row_start)
    k_part = dequantize(kv_codes[0], kv_scodes[0], kv_second[0], row_start)
    v_part = dequantize(kv_codes[1], kv_scodes[1], kv_second[1], row_start)
    o_part = dequantize(o_codes, o_scodes, o_second, row_start)
    query_matrix, key_matrix, value_matrix, output_matrix = (
        lax.all_gather(q_part, "ctx", axis=0, tiled=True),
        lax.all_gather(k_part, "ctx", axis=0, tiled=True),
        lax.all_gather(v_part, "ctx", axis=0, tiled=True),
        lax.all_gather(o_part, "ctx", axis=0, tiled=True),
    )
    whole_tokens = lax.all_gather(tokens, "tp", axis=1, tiled=True)
    wide = whole_tokens.astype(jnp.float32)
    row_scale = lax.rsqrt(jnp.mean(wide * wide, axis=1, keepdims=True) + EPSILON)
    normalized_input = (wide * row_scale * in_gain).astype(jnp.bfloat16)
    query_lowrank = jnp.dot(normalized_input, q_down, preferred_element_type=jnp.float32).astype(
        jnp.bfloat16
    )
    key_lowrank = jnp.dot(normalized_input, kv_down[0], preferred_element_type=jnp.float32).astype(
        jnp.bfloat16
    )
    value_lowrank = jnp.dot(
        normalized_input, kv_down[1], preferred_element_type=jnp.float32
    ).astype(jnp.bfloat16)
    query_rows = jnp.dot(
        normalized_input, query_matrix, preferred_element_type=jnp.float32
    ) + ADAPTER_SCALE * jnp.dot(query_lowrank, query_up, preferred_element_type=jnp.float32)
    key = jnp.dot(
        normalized_input, key_matrix, preferred_element_type=jnp.float32
    ) + ADAPTER_SCALE * jnp.dot(key_lowrank, key_value_up[0], preferred_element_type=jnp.float32)
    value_total = jnp.dot(
        normalized_input, value_matrix, preferred_element_type=jnp.float32
    ) + ADAPTER_SCALE * jnp.dot(value_lowrank, key_value_up[1], preferred_element_type=jnp.float32)
    value_rows = value_total.astype(jnp.bfloat16)
    query_pos = ctx_rank * count + jnp.arange(count, dtype=jnp.int32)
    key_pos = ctx_rank * count - WINDOW_TOKENS + jnp.arange(WINDOW_TOKENS + count, dtype=jnp.int32)
    cosine, sine = rope_tables(query_pos)
    q_heads = query_rows.reshape(count, q_heads_here, HEAD_SIZE)
    q_normed, q_scale = head_norm(q_heads, query_gain)
    q_rot = rotate(q_normed, cosine, sine).astype(jnp.bfloat16)
    key_head_rows = key.reshape(count, kv_heads_here, HEAD_SIZE)
    k_normed, k_scale = head_norm(key_head_rows, key_gain)
    k_rot = rotate(k_normed, cosine, sine).astype(jnp.bfloat16)
    piece_rows = min(WINDOW_TOKENS, count)
    pieces = WINDOW_TOKENS // piece_rows
    stacked = jnp.stack([k_rot.reshape(count, kv_width), value_rows])
    arrived = []
    for offset in range(pieces, 0, -1):
        arrived.append(from_behind(stacked, "ctx", offset))
    window = jnp.concatenate(arrived + [stacked], axis=1)
    window_keys = window[0].reshape(WINDOW_TOKENS + count, kv_heads_here, HEAD_SIZE)
    window_values = window[1].reshape(WINDOW_TOKENS + count, kv_heads_here, HEAD_SIZE)
    attended_rows = attention_forward(q_rot, window_keys, window_values, query_pos, key_pos)
    low_part = jnp.dot(attended_rows, output_down, preferred_element_type=jnp.float32)
    out_part = jnp.dot(attended_rows, output_matrix.T, preferred_element_type=jnp.float32)
    gain_mine = lax.dynamic_slice_in_dim(post_gain, column_start, share, 0)
    output_lowrank = lax.psum(low_part, "tp").astype(jnp.bfloat16)
    up_mine = lax.dynamic_slice_in_dim(output_up, column_start, share, 1)
    out_mine = lax.psum_scatter(
        out_part, "tp", scatter_dimension=1, tiled=True
    ) + ADAPTER_SCALE * jnp.dot(output_lowrank, up_mine, preferred_element_type=jnp.float32)
    square_sum = lax.psum(jnp.sum(out_mine * out_mine, axis=1, keepdims=True), "tp")
    out_scale = lax.rsqrt(square_sum / D + EPSILON)
    mixed = (tokens.astype(jnp.float32) + out_mine * out_scale * gain_mine).astype(jnp.bfloat16)
    weighted_out = out_grad.astype(jnp.float32) * gain_mine
    out_inner = lax.psum(jnp.sum(weighted_out * out_mine, axis=1, keepdims=True), "tp") / D
    grad_mine = (out_scale * weighted_out - out_scale**3 * out_mine * out_inner).astype(
        jnp.bfloat16
    )
    output_gradient = lax.all_gather(grad_mine, "tp", axis=1, tiled=True)
    output_mixture = jnp.dot(
        output_gradient, output_up.T, preferred_element_type=jnp.float32
    ).astype(jnp.bfloat16)
    output_up_gradient = ADAPTER_SCALE * jnp.dot(
        output_lowrank.T, output_gradient, preferred_element_type=jnp.float32
    )
    output_down_gradient = ADAPTER_SCALE * jnp.dot(
        attended_rows.T, output_mixture, preferred_element_type=jnp.float32
    )
    output_down_gradient, output_up_gradient = lax.psum(
        (output_down_gradient, output_up_gradient), "ctx"
    )
    attended_gradient = (
        jnp.dot(output_gradient, output_matrix, preferred_element_type=jnp.float32)
        + ADAPTER_SCALE * jnp.dot(output_mixture, output_down.T, preferred_element_type=jnp.float32)
    ).astype(jnp.bfloat16)
    query_grad, key_window_grad, value_window_grad = attention_backward(
        q_rot, window_keys, window_values, attended_gradient, query_pos, key_pos
    )
    window_grad = jnp.stack(
        [
            key_window_grad.reshape(WINDOW_TOKENS + count, kv_width),
            value_window_grad.reshape(WINDOW_TOKENS + count, kv_width),
        ]
    )
    front_rows = window_grad[:, :WINDOW_TOKENS]
    own = window_grad[:, WINDOW_TOKENS:]
    returned = jnp.zeros((2, piece_rows, kv_width), jnp.float32)
    for offset in range(1, pieces + 1):
        piece = front_rows[:, (pieces - offset) * piece_rows : (pieces - offset + 1) * piece_rows]
        returned = returned + from_behind(piece, "ctx", -offset)
    own = jnp.concatenate([own[:, : count - piece_rows], own + returned], axis=1)
    q_norm_grad = unrotate(query_grad, cosine, sine)
    k_norm_grad = unrotate(own[0].reshape(count, kv_heads_here, HEAD_SIZE), cosine, sine)
    query_gradient_lowrank = (
        head_norm_back(q_heads, q_scale, query_gain, q_norm_grad)
        .reshape(count, q_width)
        .astype(jnp.bfloat16)
    )
    key_gradient_lowrank = (
        head_norm_back(key_head_rows, k_scale, key_gain, k_norm_grad)
        .reshape(count, kv_width)
        .astype(jnp.bfloat16)
    )
    value_gradient_lowrank = own[1].astype(jnp.bfloat16)
    query_mixture = jnp.dot(query_gradient_lowrank, query_up.T, preferred_element_type=jnp.float32)
    key_mixture = jnp.dot(
        key_gradient_lowrank, key_value_up[0].T, preferred_element_type=jnp.float32
    )
    value_mixture = jnp.dot(
        value_gradient_lowrank, key_value_up[1].T, preferred_element_type=jnp.float32
    )
    into_part = jnp.dot(query_gradient_lowrank, query_matrix.T, preferred_element_type=jnp.float32)
    into_part = into_part + jnp.dot(
        key_gradient_lowrank, key_matrix.T, preferred_element_type=jnp.float32
    )
    into_part = into_part + jnp.dot(
        value_gradient_lowrank, value_matrix.T, preferred_element_type=jnp.float32
    )
    query_mixture, key_mixture, value_mixture = lax.psum(
        (query_mixture, key_mixture, value_mixture), "tp"
    )
    query_mixture = query_mixture.astype(jnp.bfloat16)
    key_mixture = key_mixture.astype(jnp.bfloat16)
    value_mixture = value_mixture.astype(jnp.bfloat16)
    into_mine = lax.psum_scatter(into_part, "tp", scatter_dimension=1, tiled=True)
    q_down_mine = lax.dynamic_slice_in_dim(q_down, column_start, share, 0)
    k_down_mine = lax.dynamic_slice_in_dim(kv_down[0], column_start, share, 0)
    v_down_mine = lax.dynamic_slice_in_dim(kv_down[1], column_start, share, 0)
    adapter_term = (
        jnp.dot(query_mixture, q_down_mine.T, preferred_element_type=jnp.float32)
        + jnp.dot(key_mixture, k_down_mine.T, preferred_element_type=jnp.float32)
        + jnp.dot(value_mixture, v_down_mine.T, preferred_element_type=jnp.float32)
    )
    normalized_gradient = into_mine + ADAPTER_SCALE * adapter_term
    in_gain_mine = lax.dynamic_slice_in_dim(in_gain, column_start, share, 0)
    weighted_in = normalized_gradient * in_gain_mine
    wide_mine = tokens.astype(jnp.float32)
    in_inner = lax.psum(jnp.sum(weighted_in * wide_mine, axis=1, keepdims=True), "tp") / D
    tokens_grad = (
        out_grad.astype(jnp.float32) + row_scale * weighted_in - row_scale**3 * wide_mine * in_inner
    )
    in_projection = float(D) ** 0.5 * row_scale * in_inner
    query_down_gradient = ADAPTER_SCALE * jnp.dot(
        normalized_input.T, query_mixture, preferred_element_type=jnp.float32
    )
    key_value_down_gradient = jnp.stack(
        [
            ADAPTER_SCALE
            * jnp.dot(normalized_input.T, key_mixture, preferred_element_type=jnp.float32),
            ADAPTER_SCALE
            * jnp.dot(normalized_input.T, value_mixture, preferred_element_type=jnp.float32),
        ]
    )
    query_up_gradient = ADAPTER_SCALE * jnp.dot(
        query_lowrank.T, query_gradient_lowrank, preferred_element_type=jnp.float32
    )
    key_value_up_gradient = jnp.stack(
        [
            ADAPTER_SCALE
            * jnp.dot(key_lowrank.T, key_gradient_lowrank, preferred_element_type=jnp.float32),
            ADAPTER_SCALE
            * jnp.dot(value_lowrank.T, value_gradient_lowrank, preferred_element_type=jnp.float32),
        ]
    )
    query_down_gradient, key_value_down_gradient, query_up_gradient, key_value_up_gradient = (
        lax.psum(
            (
                query_down_gradient,
                key_value_down_gradient,
                query_up_gradient,
                key_value_up_gradient,
            ),
            "ctx",
        )
    )
    return (
        mixed,
        tokens_grad,
        query_down_gradient,
        query_up_gradient,
        key_value_down_gradient,
        key_value_up_gradient,
        output_down_gradient,
        output_up_gradient,
        in_projection,
    )


def solution(mesh):
    placed = (
        P("ctx", "tp"),
        P("ctx", "tp"),
        P(),
        P(),
        P(),
        P(),
        P("ctx", "tp"),
        P("ctx", "tp"),
        P(None, "tp"),
        P(None, "ctx", "tp"),
        P(None, "ctx", "tp"),
        P(None, None, "tp"),
        P("ctx", "tp"),
        P("ctx", "tp"),
        P(None, "tp"),
        P(),
        P(None, "tp"),
        P(),
        P(None, None, "tp"),
        P("tp", None),
        P(),
    )
    return jax.shard_map(
        on_device,
        mesh=mesh,
        in_specs=placed,
        out_specs=(
            P("ctx", "tp"),
            P("ctx", "tp"),
            P(),
            P(None, "tp"),
            P(),
            P(None, None, "tp"),
            P("tp", None),
            P(),
            P("ctx", None),
        ),
        check_vma=False,
    )
```

profile of v0, /device:TPU:12, one launch (start us, length us, event | category | flops | bytes accessed | tf_op | source)
XLA Modules:
  0.0 805.1 jit_solution(1768596731163003433)
XLA Ops:
  27.8 9.2 %all-gather.7.cloned.1.call-done = bf16[256,5376]{0,1:T(8,128)(2,1)} async-done(((bf16[256,1344]{0,1:T(8,128)(2,1)}), bf16[256,5376]{0,1:T(8,128)(2,1)}) %all-gather.7.cloned.1.call-update) | async-done | bytes 2752528 | tf_op jit(solution)/shard_map/all_gather | solution.py:186
  37.0 2.7 fusion.3
  40.3 2.3 fusion.5
  43.6 51.3 %all-gather.9.cloned.1.call-done = bf16[5376,256]{1,0:T(8,128)(2,1)} async-done(((bf16[672,256]{1,0:T(8,128)(2,1)}), bf16[5376,256]{1,0:T(8,128)(2,1)}) %all-gather.9.cloned.1.call-update) | async-done | bytes 2752528 | tf_op jit(solution)/shard_map/all_gather | solution.py:182
  94.9 3.1 fusion.120
  99.5 52.8 %all-gather.11.cloned.1.call-done = bf16[5376,256]{1,0:T(8,128)(2,1)} async-done(((bf16[672,256]{1,0:T(8,128)(2,1)}), bf16[5376,256]{1,0:T(8,128)(2,1)}) %all-gather.11.cloned.1.call-update) | async-done | bytes 2752528 | tf_op jit(solution)/shard_map/all_gather | solution.py:183
  152.3 3.1 fusion.121
  155.6 2.9 collective-permute-start
  158.5 2.2 collective-permute-start.1
  163.1 2.7 collective-permute-start.3
  165.8 20.6 %collective-permute-done = bf16[2,256,256]{1,2,0:T(8,128)(2,1)S(1)} collective-permute-done((bf16[2,256,256]{1,2,0:T(8,128)(2,1)S(1)}, bf16[2,256,256]{1,2,0:T(8,128)(2,1)S(1)}, u32[]{:S(2)}, u32[]{:S(2)}) %collective-permute-start) | collective-permute-done | bytes 262176 | tf_op jit(solution)/shard_map/ppermute | solution.py:40
  186.4 16.6 %collective-permute-done.1 = bf16[2,256,256]{1,2,0:T(8,128)(2,1)S(1)} collective-permute-done((bf16[2,256,256]{1,2,0:T(8,128)(2,1)S(1)}, bf16[2,256,256]{1,2,0:T(8,128)(2,1)S(1)}, u32[]{:S(2)}, u32[]{:S(2)}) %collective-permute-start.1) | collective-permute-done | bytes 262176 | tf_op jit(solution)/shard_map/ppermute | solution.py:40
  203.0 5.9 collective-permute-done.2
  208.9 15.8 %collective-permute-done.3 = bf16[2,256,256]{1,2,0:T(8,128)(2,1)S(1)} collective-permute-done((bf16[2,256,256]{1,2,0:T(8,128)(2,1)S(1)}, bf16[2,256,256]{1,2,0:T(8,128)(2,1)S(1)}, u32[]{:S(2)}, u32[]{:S(2)}) %collective-permute-start.3) | collective-permute-done | bytes 262176 | tf_op jit(solution)/shard_map/ppermute | solution.py:40
  226.0 33.0 %all-gather.13.cloned.1.call-done = bf16[5376,512]{1,0:T(8,128)(2,1)} async-done(((bf16[672,512]{1,0:T(8,128)(2,1)}), bf16[5376,512]{1,0:T(8,128)(2,1)}) %all-gather.13.cloned.1.call-update) | async-done | bytes 5505040 | tf_op jit(solution)/shard_map/all_gather | solution.py:181
  259.0 4.2 fusion.122
  273.0 5.7 fusion.14
  278.7 4.0 fusion.37
  282.7 67.9 %all-gather.15.cloned.1.call-done = bf16[5376,512]{1,0:T(8,128)(2,1)} async-done(((bf16[672,512]{1,0:T(8,128)(2,1)}), bf16[5376,512]{1,0:T(8,128)(2,1)}) %all-gather.15.cloned.1.call-update) | async-done | bytes 5505040 | tf_op jit(solution)/shard_map/all_gather | solution.py:184
  350.6 6.5 fusion.127
  359.8 10.7 %psum.91 = bf16[256,16]{0,1:T(8,128)(2,1)S(1)} all-reduce(f32[256,16]{0,1:T(8,128)} %fusion.128), channel_id=1, replica_groups=mesh['ctx'=8,'tp'=4] {'tp'}, use_global_device_ids=true, to_apply=%region_5.6 | all-reduce | flops 4096 | bytes 24576 | tf_op jit(solution)/shard_map/psum | solution.py:231
  370.4 40.0 %reduce-scatter.3.cloned.1.call-done = f32[256,1344]{0,1:T(8,128)} async-done(((f32[256,5376]{0,1:T(8,128)}), f32[256,1344]{0,1:T(8,128)}) %reduce-scatter.3.cloned.1.call-update) | async-done | bytes 1376272 | tf_op jit(solution)/shard_map/reduce_scatter | solution.py:233
  410.4 3.9 fusion.24
  414.3 6.6 all-reduce.3
  422.3 3.3 fusion.23
  429.8 22.7 %all-gather.17.cloned.1.call-done = bf16[256,5376]{0,1:T(8,128)(2,1)} async-done(((bf16[256,1344]{0,1:T(8,128)(2,1)}), bf16[256,5376]{0,1:T(8,128)(2,1)}) %all-gather.17.cloned.1.call-update) | async-done | bytes 2752528 | tf_op jit(solution)/shard_map/all_gather | solution.py:244
  452.5 5.1 fusion.123
  461.1 4.4 fusion.124
  465.5 9.4 %fusion.17 = f32[2,128,2,256]{3,1,2,0:T(8,128)} fusion(bf16[1280,2,128,1]{0,2,3,1:T(8,128)(2,1)} %bitcast.278, f32[2,2,256,1280]{2,3,1,0:T(8,128)} %fusion.14, f32[2,1280,256,2]{2,1,3,0:T(8,128)} %fusion.124), kind=kOutput, calls=%fused_computation.39 | convolution fusion | flops 342100224 | bytes 11665408 | tf_op jit(solution)/shard_map/kgtl,lkd->tkgd/dot_general | solution.py:134
  475.0 10.1 %fusion.16 = f32[2,128,1280,1]{2,1,3,0:T(8,128)} fusion(f32[2,2,256,1280]{2,3,1,0:T(8,128)} %fusion.14, f32[2,1280,256,2]{2,1,3,0:T(8,128)} %fusion.124, bf16[256,2,2,64]{3,0,2,1:T(8,128)(2,1)} %bitcast.281, bf16[256,2,2,64]{3,0,2,1:T(8,128)(2,1)} %bitcast.283), kind=kOutput, calls=%fused_computation.38 | convolution fusion | flops 342624512 | bytes 12058624 | tf_op jit(solution)/shard_map/kgtl,tkgd->lkd/dot_general | solution.py:137
  485.0 4.7 fusion.29
  490.6 1.9 copy.295
  492.5 2.0 copy.294
  499.1 2.4 collective-permute-start.6
  503.5 2.2 collective-permute-start.5
  508.7 6.7 collective-permute-done.7
  515.4 11.2 %collective-permute-done.6 = f32[2,256,256]{1,2,0:T(8,128)S(1)} collective-permute-done((f32[2,256,256]{1,2,0:T(8,128)S(1)}, f32[2,256,256]{1,2,0:T(8,128)S(1)}, u32[]{:S(2)}, u32[]{:S(2)}) %collective-permute-start.6) | collective-permute-done | bytes 524320 | tf_op jit(solution)/shard_map/ppermute | solution.py:40
  526.7 32.8 %collective-permute-done.4 = f32[2,256,256]{1,2,0:T(8,128)S(1)} collective-permute-done((f32[2,256,256]{1,2,0:T(8,128)S(1)}, f32[2,256,256]{1,2,0:T(8,128)S(1)}, u32[]{:S(2)}, u32[]{:S(2)}) %collective-permute-start.4) | collective-permute-done | bytes 524320 | tf_op jit(solution)/shard_map/ppermute | solution.py:40
  563.2 3.3 convolution_add_fusion
  571.0 3.4 convolution_multiply_fusion
  574.7 10.6 %all-reduce.2 = (bf16[256,16]{0,1:T(8,128)(2,1)S(1)}, bf16[256,16]{0,1:T(8,128)(2,1)S(1)}, bf16[256,16]{0,1:T(8,128)(2,1)S(1)}) all-reduce(f32[256,16]{0,1:T(8,128)S(1)} %fusion.126, f32[256,16]{0,1:T(8,128)S(1)} %fusion.77, f32[256,16]{0,1:T(8,128)S(1)} %fusion.74), channel_id=1, replica_groups=mesh['ctx'=8,'tp'=4] {'tp'}, use_global_device_ids=true, to_apply=%region_14.15 | all-reduce | flops 12288 | bytes 73728 | tf_op jit(solution)/shard_map/psum | solution.py:304
  591.9 2.4 convolution_add_fusion.3
  594.4 33.1 %reduce-scatter.5.cloned.1.call-done = f32[256,1344]{0,1:T(8,128)} async-done(((f32[256,5376]{0,1:T(8,128)}), f32[256,1344]{0,1:T(8,128)}) %reduce-scatter.5.cloned.1.call-update) | async-done | bytes 1376272 | tf_op jit(solution)/shard_map/reduce_scatter | solution.py:310
  627.5 2.7 fusion.28
  630.2 6.0 psum.97
  638.1 63.8 %all-reduce.7.cloned.1.call-done = (f32[16,512]{1,0:T(8,128)}, f32[2,16,256]{2,1,0:T(8,128)}, f32[512,16]{0,1:T(8,128)}) async-done(((f32[16,512]{1,0:T(8,128)}, f32[2,16,256]{2,1,0:T(8,128)}, f32[512,16]{0,1:T(8,128)}), (f32[16,512]{1,0:T(8,128)}, f32[2,16,256]{2,1,0:T(8,128)}, f32[512,16]{0,1:T(8,128)})) %all-reduce.7.cloned.1.call-update) | async-done | bytes 98320 | tf_op jit(solution)/shard_map/psum | solution.py:351
  702.0 88.9 %all-reduce.9.cloned.1.call-done = (f32[5376,16]{0,1:T(8,128)}, f32[2,5376,16]{1,2,0:T(8,128)}, f32[16,5376]{1,0:T(8,128)}) async-done(((f32[5376,16]{0,1:T(8,128)}, f32[2,5376,16]{1,2,0:T(8,128)}, f32[16,5376]{1,0:T(8,128)}), (f32[5376,16]{0,1:T(8,128)}, f32[2,5376,16]{1,2,0:T(8,128)}, f32[16,5376]{1,0:T(8,128)})) %all-reduce.9.cloned.1.call-update) | async-done | bytes 1376272 | tf_op jit(solution)/shard_map/psum | solution.py:351
  794.1 2.0 copy.318
  (239 shorter events, 81.0 us)
Async XLA Ops:
  7.2 403.2 %copy-start = (bf16[16,5376]{1,0:T(8,128)(2,1)S(1)}, bf16[16,5376]{1,0:T(8,128)(2,1)}, u32[]{:S(2)}) copy-start(bf16[16,5376]{1,0:T(8,128)(2,1)} %param.41) | copy-start | bytes 516100
  7.2 29.8 %all-gather.7.cloned.1.call-start = ((), (), s32[]{:S(2)}) async-start(), calls=%async_computation.2 | async-start | bytes 3440640 | tf_op jit(solution)/shard_map/all_gather | solution.py:186
  7.9 86.9 %all-gather.9.cloned.1.call-start = ((), (), s32[]{:S(2)}) async-start(), calls=%async_computation.3 | async-start | bytes 3096576 | tf_op jit(solution)/shard_map/all_gather | solution.py:182
  11.9 140.4 %all-gather.11.cloned.1.call-start = ((), (), s32[]{:S(2)}) async-start(), calls=%async_computation.4 | async-start | bytes 3096576 | tf_op jit(solution)/shard_map/all_gather | solution.py:183
  14.4 244.6 %all-gather.13.cloned.1.call-start = ((), (), s32[]{:S(2)}) async-start(), calls=%async_computation.5 | async-start | bytes 6193152 | tf_op jit(solution)/shard_map/all_gather | solution.py:181
  19.6 331.1 %all-gather.15.cloned.1.call-start = ((), (), s32[]{:S(2)}) async-start(), calls=%async_computation.6 | async-start | bytes 6193152 | tf_op jit(solution)/shard_map/all_gather | solution.py:184
  24.8 385.6 %reduce-scatter.3.cloned.1.call-start = ((), (), s32[]{:S(2)}) async-start(), calls=%async_computation.7 | async-start | bytes 6881280 | tf_op jit(solution)/shard_map/reduce_scatter | solution.py:233
  25.9 13.7 %copy-start.16 = (f32[256,64]{1,0:T(8,128)}, f32[256,64]{1,0:T(8,128)S(1)}, u32[]{:S(2)}) copy-start(f32[256,64]{1,0:T(8,128)S(1)} %get-tuple-element.54) | copy-start | bytes 196612
  25.9 13.7 %copy-start.18 = (f32[256,64]{1,0:T(8,128)}, f32[256,64]{1,0:T(8,128)S(1)}, u32[]{:S(2)}) copy-start(f32[256,64]{1,0:T(8,128)S(1)} %get-tuple-element.55) | copy-start | bytes 196612
  26.1 72.9 %copy-start.21 = (f32[256,64]{0,1:T(8,128)}, f32[256,64]{0,1:T(8,128)S(1)}, u32[]{:S(2)}) copy-start(f32[256,64]{0,1:T(8,128)S(1)} %copy.217) | copy-start | bytes 196612
  26.1 14.2 %copy-start.32 = (f32[5376]{0:T(1024)S(1)}, f32[5376]{0:T(1024)}, u32[]{:S(2)}) copy-start(f32[5376]{0:T(1024)} %param.23) | copy-start | bytes 64516
  43.5 54.4 %copy-start.29 = (bf16[2,16,256]{2,1,0:T(8,128)(2,1)S(1)}, bf16[2,16,256]{2,1,0:T(8,128)(2,1)}, u32[]{:S(2)}) copy-start(bf16[2,16,256]{2,1,0:T(8,128)(2,1)} %param.39) | copy-start | bytes 49156
  43.5 55.3 %copy-start.45 = (f32[128]{0:T(128)S(1)}, f32[128]{0:T(128)}, u32[]{:S(2)}) copy-start(f32[128]{0:T(128)} %param.25) | copy-start | bytes 1540
  99.4 63.2 %copy-start.26 = (bf16[5376,16]{0,1:T(8,128)(2,1)S(1)}, bf16[5376,16]{0,1:T(8,128)(2,1)}, u32[]{:S(2)}) copy-start(bf16[5376,16]{0,1:T(8,128)(2,1)} %param.36) | copy-start | bytes 516100
  155.6 30.8 %collective-permute-start = (bf16[2,256,256]{1,2,0:T(8,128)(2,1)S(1)}, bf16[2,256,256]{1,2,0:T(8,128)(2,1)S(1)}, u32[]{:S(2)}, u32[]{:S(2)}) collective-permute-start(bf16[2,256,256]{1,2,0:T(8,128)(2,1)S(1)} %pad_maximum_fusion.3), channel_id=1, source_target_pairs={{0,16},{4,20},{8,24},{12,28},{1,17},{5,21},{9,25},{13,29},{2,18},{... | collective-permute-start | bytes 786440 | tf_op jit(solution)/shard_map/ppermute | solution.py:40
  158.5 44.4 %collective-permute-start.1 = (bf16[2,256,256]{1,2,0:T(8,128)(2,1)S(1)}, bf16[2,256,256]{1,2,0:T(8,128)(2,1)S(1)}, u32[]{:S(2)}, u32[]{:S(2)}) collective-permute-start(bf16[2,256,256]{1,2,0:T(8,128)(2,1)S(1)} %pad_maximum_fusion.3), channel_id=1, source_target_pairs={{0,12},{4,16},{8,20},{12,24},{16,28},{1,13},{5,17},{9,21},{13,25},... | collective-permute-start | bytes 786440 | tf_op jit(solution)/shard_map/ppermute | solution.py:40
  160.7 48.2 %collective-permute-start.2 = (bf16[2,256,256]{1,2,0:T(8,128)(2,1)S(1)}, bf16[2,256,256]{1,2,0:T(8,128)(2,1)S(1)}, u32[]{:S(2)}, u32[]{:S(2)}) collective-permute-start(bf16[2,256,256]{1,2,0:T(8,128)(2,1)S(1)} %pad_maximum_fusion.3), channel_id=1, source_target_pairs={{0,8},{4,12},{8,16},{12,20},{16,24},{20,28},{1,9},{5,13},{9,17},{1... | collective-permute-start | bytes 786440 | tf_op jit(solution)/shard_map/ppermute | solution.py:40
  163.1 61.7 %collective-permute-start.3 = (bf16[2,256,256]{1,2,0:T(8,128)(2,1)S(1)}, bf16[2,256,256]{1,2,0:T(8,128)(2,1)S(1)}, u32[]{:S(2)}, u32[]{:S(2)}) collective-permute-start(bf16[2,256,256]{1,2,0:T(8,128)(2,1)S(1)} %pad_maximum_fusion.3), channel_id=1, source_target_pairs={{0,4},{4,8},{8,12},{12,16},{16,20},{20,24},{24,28},{1,5},{5,9},{9,... | collective-permute-start | bytes 786440 | tf_op jit(solution)/shard_map/ppermute | solution.py:40
  226.0 37.1 %copy-start.27 = (bf16[16,512]{1,0:T(8,128)(2,1)S(1)}, bf16[16,512]{1,0:T(8,128)(2,1)}, u32[]{:S(2)}) copy-start(bf16[16,512]{1,0:T(8,128)(2,1)} %param.37) | copy-start | bytes 49156
  263.1 5.7 copy-start.41
  357.2 95.3 %all-gather.17.cloned.1.call-start = ((), (), s32[]{:S(2)}) async-start(), calls=%async_computation.8 | async-start | bytes 3440640 | tf_op jit(solution)/shard_map/all_gather | solution.py:244
  425.6 201.9 %reduce-scatter.5.cloned.1.call-start = ((), (), s32[]{:S(2)}) async-start(), calls=%async_computation.9 | async-start | bytes 6881280 | tf_op jit(solution)/shard_map/reduce_scatter | solution.py:310
  452.5 5.1 copy-start.2
  489.7 4.8 copy-start.17
  496.1 10.9 %slice-start = ((s8[5505024]{0:T(1024)(128)(4,1)}), s8[4194304]{0:T(1024)(128)(4,1)S(1)}, s32[]{:S(2)}) async-start(s8[5505024]{0:T(1024)(128)(4,1)} %bitcast.257), calls=%async_computation.12 | async-start | bytes 8388608
  497.4 8.6 %copy-start.23 = (f32[256,4]{1,0:T(8,128)S(1)}, f32[256,4]{1,0:T(8,128)}, u32[]{:S(2)}) copy-start(f32[256,4]{1,0:T(8,128)} %copy.268) | copy-start | bytes 12292
  497.4 8.9 %copy-start.20 = (f32[256,4]{1,0:T(8,128)S(1)}, f32[256,4]{1,0:T(8,128)}, u32[]{:S(2)}) copy-start(f32[256,4]{1,0:T(8,128)} %copy.241) | copy-start | bytes 12292
  497.4 9.6 %slice-start.1 = ((s8[5505024]{0:T(1024)(128)(4,1)}), s8[1310720]{0:T(1024)(128)(4,1)S(1)}, s32[]{:S(2)}) async-start(s8[5505024]{0:T(1024)(128)(4,1)} %bitcast.257), calls=%async_computation.13 | async-start | bytes 2621440
  497.6 9.0 %copy-start.12 = (f32[256,512]{1,0:T(8,128)S(1)}, f32[256,512]{1,0:T(8,128)}, u32[]{:S(2)}) copy-start(f32[256,512]{1,0:T(8,128)} %fusion.35) | copy-start | bytes 1572868
  497.6 9.0 %copy-start.39 = (f32[512]{0:T(512)S(1)}, f32[512]{0:T(512)}, u32[]{:S(2)}) copy-start(f32[512]{0:T(512)} %broadcast_bitcast_fusion) | copy-start | bytes 6148
  497.7 17.8 %collective-permute-start.7 = (f32[2,256,256]{1,2,0:T(8,128)S(1)}, f32[2,256,256]{1,2,0:T(8,128)S(1)}, u32[]{:S(2)}, u32[]{:S(2)}) collective-permute-start(f32[2,256,256]{1,2,0:T(8,128)S(1)} %get-tuple-element.28), channel_id=1, source_target_pairs={{16,0},{20,4},{24,8},{28,12},{17,1},{21,5},{25,9},{29,13},{18,2},{... | collective-permute-start | bytes 1572872 | tf_op jit(solution)/shard_map/ppermute | solution.py:40
  499.1 27.6 %collective-permute-start.6 = (f32[2,256,256]{1,2,0:T(8,128)S(1)}, f32[2,256,256]{1,2,0:T(8,128)S(1)}, u32[]{:S(2)}, u32[]{:S(2)}) collective-permute-start(f32[2,256,256]{1,2,0:T(8,128)S(1)} %get-tuple-element.29), channel_id=1, source_target_pairs={{12,0},{16,4},{20,8},{24,12},{28,16},{13,1},{17,5},{21,9},{25,13},... | collective-permute-start | bytes 1572872 | tf_op jit(solution)/shard_map/ppermute | solution.py:40
  501.5 57.9 %collective-permute-start.4 = (f32[2,256,256]{1,2,0:T(8,128)S(1)}, f32[2,256,256]{1,2,0:T(8,128)S(1)}, u32[]{:S(2)}, u32[]{:S(2)}) collective-permute-start(f32[2,256,256]{1,2,0:T(8,128)S(1)} %get-tuple-element.27), channel_id=1, source_target_pairs={{4,0},{8,4},{12,8},{16,12},{20,16},{24,20},{28,24},{5,1},{9,5},{13... | collective-permute-start | bytes 1572872 | tf_op jit(solution)/shard_map/ppermute | solution.py:40
  503.5 56.0 %collective-permute-start.5 = (f32[2,256,256]{1,2,0:T(8,128)S(1)}, f32[2,256,256]{1,2,0:T(8,128)S(1)}, u32[]{:S(2)}, u32[]{:S(2)}) collective-permute-start(f32[2,256,256]{1,2,0:T(8,128)S(1)} %get-tuple-element.26), channel_id=1, source_target_pairs={{8,0},{12,4},{16,8},{20,12},{24,16},{28,20},{9,1},{13,5},{17,9},{2... | collective-permute-start | bytes 1572872 | tf_op jit(solution)/shard_map/ppermute | solution.py:40
  508.7 51.0 %copy-start.22 = (f32[256,64]{0,1:T(8,128)S(1)}, f32[256,64]{0,1:T(8,128)}, u32[]{:S(2)}) copy-start(f32[256,64]{0,1:T(8,128)} %copy-done.21) | copy-start | bytes 196612
  508.7 51.0 %copy-start.15 = (f32[256,256]{0,1:T(8,128)S(1)}, f32[256,256]{0,1:T(8,128)}, u32[]{:S(2)}) copy-start(f32[256,256]{0,1:T(8,128)} %copy-done.14) | copy-start | bytes 786436
  508.7 51.0 %copy-start.46 = (f32[128]{0:T(128)S(1)}, f32[128]{0:T(128)}, u32[]{:S(2)}) copy-start(f32[128]{0:T(128)} %param.25) | copy-start | bytes 1540
  566.6 135.4 %all-reduce.7.cloned.1.call-start = ((), (), s32[]{:S(2)}) async-start(), calls=%async_computation.10 | async-start | bytes 196608 | tf_op jit(solution)/shard_map/psum | solution.py:351
  590.5 200.4 %all-reduce.9.cloned.1.call-start = ((), (), s32[]{:S(2)}) async-start(), calls=%async_computation.11 | async-start | bytes 2752512 | tf_op jit(solution)/shard_map/psum | solution.py:351
  591.9 35.6 %copy-start.5 = (bf16[256,1344]{0,1:T(8,128)(2,1)S(1)}, bf16[256,1344]{0,1:T(8,128)(2,1)}, u32[]{:S(2)}) copy-start(bf16[256,1344]{0,1:T(8,128)(2,1)} %param.21) | copy-start | bytes 2064388
  627.5 8.7 %copy-start.43 = (f32[256]{0:T(256)S(1)}, f32[256]{0:T(256)}, u32[]{:S(2)}) copy-start(f32[256]{0:T(256)} %get-tuple-element.58) | copy-start | bytes 3076
  627.5 9.2 %copy-start.8 = (bf16[256,1344]{0,1:T(8,128)(2,1)S(1)}, bf16[256,1344]{0,1:T(8,128)(2,1)}, u32[]{:S(2)}) copy-start(bf16[256,1344]{0,1:T(8,128)(2,1)} %param.22) | copy-start | bytes 2064388
  627.5 9.2 %copy-start.38 = (f32[256]{0:T(256)S(1)}, f32[256]{0:T(256)}, u32[]{:S(2)}) copy-start(f32[256]{0:T(256)} %copy-done.37) | copy-start | bytes 3076
  627.5 9.2 %copy-start.44 = (f32[256]{0:T(256)S(1)}, f32[256]{0:T(256)}, u32[]{:S(2)}) copy-start(f32[256]{0:T(256)} %get-tuple-element.59) | copy-start | bytes 3076
  636.7 161.3 %copy-start.1 = (bf16[16,5376]{1,0:T(8,128)(2,1)S(1)}, bf16[16,5376]{1,0:T(8,128)(2,1)}, u32[]{:S(2)}) copy-start(bf16[16,5376]{1,0:T(8,128)(2,1)} %param.41) | copy-start | bytes 516100
  702.0 94.1 %copy-start.34 = (f32[2,16,256]{2,1,0:T(8,128)S(1)}, f32[2,16,256]{2,1,0:T(8,128)}, u32[]{:S(2)}) copy-start(f32[2,16,256]{2,1,0:T(8,128)} %get-tuple-element.73) | copy-start | bytes 98308
  702.0 94.7 %copy-start.33 = (f32[512,16]{0,1:T(8,128)S(1)}, f32[512,16]{0,1:T(8,128)}, u32[]{:S(2)}) copy-start(f32[512,16]{0,1:T(8,128)} %get-tuple-element.74) | copy-start | bytes 98308
  790.9 6.4 copy-start.25
  (26 other events, 55.6 us)
Sparse Core Ops, SparseCore 0:
  9.6 27.3 all-gather.6
  39.7 55.0 all-gather.8
  97.6 54.5 all-gather.10
  154.9 104.0 all-gather.12
  261.6 89.0 all-gather.14
  357.3 53.0 reduce-scatter.2
  425.7 26.7 all-gather.16
  566.7 60.7 reduce-scatter.4
  631.8 70.1 all-reduce.6
  706.2 84.6 all-reduce.8
where the time goes:
time: 814 us; the launch traced here: 805 us
  waiting for transfers between devices  573 us (70%)
  matrix products  92.9 us (11%)
  local copies, waits for them, and re-layouts  41.2 us (5%)
  blocking collectives  33.8 us (4%)
  other arithmetic  29.9 us (4%)
  starting transfers between devices  18.8 us (2%)
  between operations  15.4 us (2%)
    psum x2, waiting for transfers between devices, on_device(): lax.psum((query_down_gradient, key_value_down_gradient, query_up_gradient...  153 us
    ppermute x8, waiting for transfers between devices, from_behind(): return lax.ppermute(shard, axis, pairs)  110 us
    all_gather x1, waiting for transfers between devices, on_device(): lax.all_gather(o_part, 'ctx', axis=0, tiled=True)  67.9 us
    all_gather x1, waiting for transfers between devices, on_device(): lax.all_gather(v_part, 'ctx', axis=0, tiled=True)  52.8 us
    all_gather x1, waiting for transfers between devices, on_device(): lax.all_gather(k_part, 'ctx', axis=0, tiled=True)  51.3 us
    reduce_scatter x1, waiting for transfers between devices, on_device(): lax.psum_scatter(out_part, 'tp', scatter_dimension=1, tiled=True)  40 us
    reduce_scatter x1, waiting for transfers between devices, on_device(): lax.psum_scatter(into_part, 'tp', scatter_dimension=1, tiled=True)  33.1 us
    all_gather x1, waiting for transfers between devices, on_device(): lax.all_gather(q_part, 'ctx', axis=0, tiled=True)  33 us
  transfers between devices with their start and end apart: 18, of which 17 were waited for; matrix products, arithmetic and copies ran while one was open for 11% of the time, Pallas kernels for 0%

commit v1 on v0

--- a/solution.py
+++ b/solution.py
@@ -1,6 +1,10 @@
+import functools
+
 import jax
 import jax.numpy as jnp
 from jax import lax
+from jax.experimental import pallas as pl
+from jax.experimental.pallas import tpu as pltpu
 from jax.sharding import PartitionSpec as P
 
 D = 5376
@@ -38,6 +42,185 @@
     devices = lax.axis_size(axis)
     pairs = [(i, i + by) for i in range(devices) if 0 <= i + by < devices]
     return lax.ppermute(shard, axis, pairs)
+
+
+MESH = pl.DeviceIdType.MESH
+
+
+def ring_place(index, devices):
+    odd = index % 2
+    return (1 - odd) * (index // 2) + odd * (devices - 1 - index // 2)
+
+
+def ring_index(place, devices):
+    back = place // (devices // 2)
+    return (1 - back) * 2 * place + back * (2 * (devices - 1 - place) + 1)
+
+
+def gather_kernel(devices, chunks, a_ref, b_ref, a_out, b_out, own_sem, send_sem, recv_sem):
+    me = lax.axis_index("ctx")
+    place = ring_place(me, devices)
+    right = ring_index((place + 1) % devices, devices)
+    left = ring_index((place + devices - 1) % devices, devices)
+    barrier = pltpu.get_barrier_semaphore()
+    for neighbour in (left, right):
+        pl.semaphore_signal(barrier, inc=1, device_id={"ctx": neighbour}, device_id_type=MESH)
+    pl.semaphore_wait(barrier, 2)
+    own = []
+    for way, (source, target) in enumerate(((a_ref, a_out), (b_ref, b_out))):
+        own.append(pltpu.make_async_copy(source, target.at[me], own_sem.at[way]))
+        own[-1].start()
+    rows = a_ref.shape[0] // chunks
+    copies = {}
+    for step in range(devices - 1):
+        for chunk in range(chunks):
+            part = pl.ds(chunk * rows, rows)
+            for way, (source, target) in enumerate(((a_ref, a_out), (b_ref, b_out))):
+                if step > 0:
+                    copies[step - 1, chunk, way].wait_recv()
+                shift = devices - step if way == 0 else step
+                owner = ring_index((place + shift) % devices, devices)
+                copy = pltpu.make_async_remote_copy(
+                    src_ref=source.at[part] if step == 0 else target.at[owner, part],
+                    dst_ref=target.at[owner, part],
+                    send_sem=send_sem.at[way, step * chunks + chunk],
+                    recv_sem=recv_sem.at[way, step * chunks + chunk],
+                    device_id={"ctx": right if way == 0 else left},
+                    device_id_type=MESH,
+                )
+                copy.start()
+                copies[step, chunk, way] = copy
+    for chunk in range(chunks):
+        for way in range(2):
+            copies[devices - 2, chunk, way].wait_recv()
+    for copy in copies.values():
+        copy.wait_send()
+    for copy in own:
+        copy.wait()
+
+
+def gather_pair(a, b, collective_id):
+    devices = lax.axis_size("ctx")
+    rows = a.shape[0]
+    chunks = 3 if rows % 48 == 0 else 1
+    count = (devices - 1) * chunks
+    sent = (devices - 1) * (a.size + b.size) * 2
+    gathered = pl.pallas_call(
+        functools.partial(gather_kernel, devices, chunks),
+        out_shape=[jax.ShapeDtypeStruct((devices,) + x.shape, x.dtype) for x in (a, b)],
+        in_specs=[pl.BlockSpec(memory_space=pl.ANY)] * 2,
+        out_specs=[pl.BlockSpec(memory_space=pl.ANY)] * 2,
+        scratch_shapes=[
+            pltpu.SemaphoreType.DMA((2,)),
+            pltpu.SemaphoreType.DMA((2, count)),
+            pltpu.SemaphoreType.DMA((2, count)),
+        ],
+        cost_estimate=pl.CostEstimate(flops=0, bytes_accessed=sent * 20, transcendentals=0),
+        compiler_params=pltpu.CompilerParams(collective_id=collective_id, has_side_effects=True),
+    )(a, b)
+    return [x.reshape(devices * rows, x.shape[2]) for x in gathered]
+
+
+def reduce_kernel(
+    devices, sharers, split, g_ref, down_ref, up_ref, slots, summed, gathered, sems, side_sems
+):
+    me = lax.axis_index("ctx")
+    side = lax.axis_index("tp")
+    rows = g_ref.shape[0] // devices
+    barrier = pltpu.get_barrier_semaphore()
+    for k in range(1, devices):
+        pl.semaphore_signal(
+            barrier, inc=1, device_id={"ctx": (me + k) % devices}, device_id_type=MESH
+        )
+    for k in range(1, sharers):
+        pl.semaphore_signal(
+            barrier, inc=1, device_id={"tp": (side + k) % sharers}, device_id_type=MESH
+        )
+    pl.semaphore_wait(barrier, devices + sharers - 2)
+    first = []
+    for k in range(1, devices):
+        other = (me + k) % devices
+        copy = pltpu.make_async_remote_copy(
+            src_ref=g_ref.at[pl.ds(pl.multiple_of(other * rows, rows), rows)],
+            dst_ref=slots.at[k],
+            send_sem=sems.at[0, k],
+            recv_sem=sems.at[1, k],
+            device_id={"ctx": other},
+            device_id_type=MESH,
+        )
+        copy.start()
+        first.append(copy)
+    total = g_ref[pl.ds(pl.multiple_of(me * rows, rows), rows), :]
+    for k in range(1, devices):
+        first[k - 1].wait_recv()
+        total = total + slots[k]
+    summed[...] = total
+    gathered[me] = total
+    second = []
+    for k in range(1, devices):
+        copy = pltpu.make_async_remote_copy(
+            src_ref=summed,
+            dst_ref=gathered.at[me],
+            send_sem=sems.at[2, k],
+            recv_sem=sems.at[3, k],
+            device_id={"ctx": (me + k) % devices},
+            device_id_type=MESH,
+        )
+        copy.start()
+        second.append(copy)
+    for copy in second:
+        copy.wait_recv()
+    third = []
+    for k in range(1, sharers):
+        copy = pltpu.make_async_remote_copy(
+            src_ref=gathered.at[:, :, pl.ds(0, split)],
+            dst_ref=down_ref.at[side],
+            send_sem=side_sems.at[0, k],
+            recv_sem=side_sems.at[1, k],
+            device_id={"tp": (side + k) % sharers},
+            device_id_type=MESH,
+        )
+        copy.start()
+        third.append(copy)
+    down_ref[side] = gathered[:, :, :split]
+    up_ref[...] = gathered[:, :, split:]
+    for copy in first + second:
+        copy.wait_send()
+    for copy in third:
+        copy.wait()
+
+
+def reduce_gradients(down, up, collective_id):
+    devices = lax.axis_size("ctx")
+    sharers = lax.axis_size("tp")
+    height, width = down.shape
+    up_shape = up.shape
+    if height % (8 * devices) or up.size % (128 * height):
+        down, up = lax.psum((down, up), "ctx")
+        return lax.all_gather(down, "tp"), up
+    up = up.reshape(height, up.size // height)
+    split = -(-width // 128) * 128
+    packed = jnp.concatenate([down, jnp.zeros((height, split - width), jnp.float32), up], axis=1)
+    rows = height // devices
+    whole = packed.shape[1]
+    down, up = pl.pallas_call(
+        functools.partial(reduce_kernel, devices, sharers, split),
+        out_shape=[
+            jax.ShapeDtypeStruct((sharers, devices, rows, split), jnp.float32),
+            jax.ShapeDtypeStruct((devices, rows, whole - split), jnp.float32),
+        ],
+        in_specs=[pl.BlockSpec(memory_space=pltpu.VMEM)],
+        out_specs=[pl.BlockSpec(memory_space=pltpu.VMEM)] * 2,
+        scratch_shapes=[
+            pltpu.VMEM((devices, rows, whole), jnp.float32),
+            pltpu.VMEM((rows, whole), jnp.float32),
+            pltpu.VMEM((devices, rows, whole), jnp.float32),
+            pltpu.SemaphoreType.DMA((4, devices)),
+            pltpu.SemaphoreType.DMA((2, sharers)),
+        ],
+        compiler_params=pltpu.CompilerParams(collective_id=collective_id, has_side_effects=True),
+    )(packed)
+    return down.reshape(sharers, height, split)[:, :, :width], up.reshape(up_shape)
 
 
 def dequantize(codes, scodes, second, row_start):
@@ -177,12 +360,11 @@
     k_part = dequantize(kv_codes[0], kv_scodes[0], kv_second[0], row_start)
     v_part = dequantize(kv_codes[1], kv_scodes[1], kv_second[1], row_start)
     o_part = dequantize(o_codes, o_scodes, o_second, row_start)
-    query_matrix, key_matrix, value_matrix, output_matrix = (
-        lax.all_gather(q_part, "ctx", axis=0, tiled=True),
-        lax.all_gather(k_part, "ctx", axis=0, tiled=True),
-        lax.all_gather(v_part, "ctx", axis=0, tiled=True),
-        lax.all_gather(o_part, "ctx", axis=0, tiled=True),
-    )
+    key_matrix, value_matrix = gather_pair(k_part, v_part, 1)
+    q_part, o_part, key_matrix, value_matrix = lax.optimization_barrier(
+        (q_part, o_part, key_matrix, value_matrix)
+    )
+    query_matrix, output_matrix = gather_pair(q_part, o_part, 2)
     whole_tokens = lax.all_gather(tokens, "tp", axis=1, tiled=True)
     wide = whole_tokens.astype(jnp.float32)
     row_scale = lax.rsqrt(jnp.mean(wide * wide, axis=1, keepdims=True) + EPSILON)
@@ -231,8 +413,8 @@
     output_lowrank = lax.psum(low_part, "tp").astype(jnp.bfloat16)
     up_mine = lax.dynamic_slice_in_dim(output_up, column_start, share, 1)
     out_mine = lax.psum_scatter(
-        out_part, "tp", scatter_dimension=1, tiled=True
-    ) + ADAPTER_SCALE * jnp.dot(output_lowrank, up_mine, preferred_element_type=jnp.float32)
+        out_part.astype(jnp.bfloat16), "tp", scatter_dimension=1, tiled=True
+    ).astype(jnp.float32) + ADAPTER_SCALE * jnp.dot(output_lowrank, up_mine, preferred_element_type=jnp.float32)
     square_sum = lax.psum(jnp.sum(out_mine * out_mine, axis=1, keepdims=True), "tp")
     out_scale = lax.rsqrt(square_sum / D + EPSILON)
     mixed = (tokens.astype(jnp.float32) + out_mine * out_scale * gain_mine).astype(jnp.bfloat16)
@@ -245,14 +427,9 @@
     output_mixture = jnp.dot(
         output_gradient, output_up.T, preferred_element_type=jnp.float32
     ).astype(jnp.bfloat16)
-    output_up_gradient = ADAPTER_SCALE * jnp.dot(
-        output_lowrank.T, output_gradient, preferred_element_type=jnp.float32
-    )
-    output_down_gradient = ADAPTER_SCALE * jnp.dot(
-        attended_rows.T, output_mixture, preferred_element_type=jnp.float32
-    )
-    output_down_gradient, output_up_gradient = lax.psum(
-        (output_down_gradient, output_up_gradient), "ctx"
+    output_up_part = jnp.dot(output_lowrank.T, grad_mine, preferred_element_type=jnp.float32)
+    output_down_part = jnp.dot(
+        output_mixture.T, attended_rows, preferred_element_type=jnp.float32
     )
     attended_gradient = (
         jnp.dot(output_gradient, output_matrix, preferred_element_type=jnp.float32)
@@ -267,12 +444,12 @@
             value_window_grad.reshape(WINDOW_TOKENS + count, kv_width),
         ]
     )
-    front_rows = window_grad[:, :WINDOW_TOKENS]
+    front_rows = window_grad[:, :WINDOW_TOKENS].astype(jnp.bfloat16)
     own = window_grad[:, WINDOW_TOKENS:]
     returned = jnp.zeros((2, piece_rows, kv_width), jnp.float32)
     for offset in range(1, pieces + 1):
         piece = front_rows[:, (pieces - offset) * piece_rows : (pieces - offset + 1) * piece_rows]
-        returned = returned + from_behind(piece, "ctx", -offset)
+        returned = returned + from_behind(piece, "ctx", -offset).astype(jnp.float32)
     own = jnp.concatenate([own[:, : count - piece_rows], own + returned], axis=1)
     q_norm_grad = unrotate(query_grad, cosine, sine)
     k_norm_grad = unrotate(own[0].reshape(count, kv_heads_here, HEAD_SIZE), cosine, sine)
@@ -307,7 +484,9 @@
     query_mixture = query_mixture.astype(jnp.bfloat16)
     key_mixture = key_mixture.astype(jnp.bfloat16)
     value_mixture = value_mixture.astype(jnp.bfloat16)
-    into_mine = lax.psum_scatter(into_part, "tp", scatter_dimension=1, tiled=True)
+    into_mine = lax.psum_scatter(
+        into_part.astype(jnp.bfloat16), "tp", scatter_dimension=1, tiled=True
+    ).astype(jnp.float32)
     q_down_mine = lax.dynamic_slice_in_dim(q_down, column_start, share, 0)
     k_down_mine = lax.dynamic_slice_in_dim(kv_down[0], column_start, share, 0)
     v_down_mine = lax.dynamic_slice_in_dim(kv_down[1], column_start, share, 0)
@@ -325,39 +504,36 @@
         out_grad.astype(jnp.float32) + row_scale * weighted_in - row_scale**3 * wide_mine * in_inner
     )
     in_projection = float(D) ** 0.5 * row_scale * in_inner
-    query_down_gradient = ADAPTER_SCALE * jnp.dot(
-        normalized_input.T, query_mixture, preferred_element_type=jnp.float32
-    )
-    key_value_down_gradient = jnp.stack(
+    normed_mine = (wide_mine * row_scale * in_gain_mine).astype(jnp.bfloat16)
+    mixtures = jnp.concatenate([query_mixture, key_mixture, value_mixture], axis=1)
+    down_part = jnp.concatenate(
+        [jnp.dot(mixtures.T, normed_mine, preferred_element_type=jnp.float32), output_up_part]
+    )
+    up_part = jnp.concatenate(
         [
-            ADAPTER_SCALE
-            * jnp.dot(normalized_input.T, key_mixture, preferred_element_type=jnp.float32),
-            ADAPTER_SCALE
-            * jnp.dot(normalized_input.T, value_mixture, preferred_element_type=jnp.float32),
-        ]
-    )
-    query_up_gradient = ADAPTER_SCALE * jnp.dot(
-        query_lowrank.T, query_gradient_lowrank, preferred_element_type=jnp.float32
-    )
+            jnp.dot(query_lowrank.T, query_gradient_lowrank, preferred_element_type=jnp.float32),
+            jnp.dot(key_lowrank.T, key_gradient_lowrank, preferred_element_type=jnp.float32),
+            jnp.dot(value_lowrank.T, value_gradient_lowrank, preferred_element_type=jnp.float32),
+            output_down_part,
+        ],
+        axis=1,
+    )
+    down_sum, up_sum = reduce_gradients(ADAPTER_SCALE * down_part, ADAPTER_SCALE * up_part, 3)
+    rank = query_up.shape[0]
+    sharers = down_sum.shape[0]
+    down_sum = down_sum.reshape(sharers, 4, rank, share)
+    down_turned = down_sum[:, :3].transpose(1, 0, 3, 2).reshape(3, sharers * share, rank)
+    query_down_gradient = down_turned[0]
+    key_value_down_gradient = down_turned[1:]
+    output_up_gradient = down_sum[:, 3].transpose(1, 0, 2).reshape(rank, sharers * share)
+    query_up_gradient = up_sum[:, :q_width]
     key_value_up_gradient = jnp.stack(
         [
-            ADAPTER_SCALE
-            * jnp.dot(key_lowrank.T, key_gradient_lowrank, preferred_element_type=jnp.float32),
-            ADAPTER_SCALE
-            * jnp.dot(value_lowrank.T, value_gradient_lowrank, preferred_element_type=jnp.float32),
+            up_sum[:, q_width : q_width + kv_width],
+            up_sum[:, q_width + kv_width : q_width + 2 * kv_width],
         ]
     )
-    query_down_gradient, key_value_down_gradient, query_up_gradient, key_value_up_gradient = (
-        lax.psum(
-            (
-                query_down_gradient,
-                key_value_down_gradient,
-                query_up_gradient,
-                key_value_up_gradient,
-            ),
-            "ctx",
-        )
-    )
+    output_down_gradient = up_sum[:, q_width + 2 * kv_width :].T
     return (
         mixed,
         tokens_grad,

time: 814 us -> 506 us (0.62)
  waiting for transfers between devices: 573 us -> 92.8 us
  Pallas kernels: 0 us -> 202 us
  matrix products: 92.9 us -> 70.6 us
    all_gather x4 -> x0, waiting for transfers between devices: 205 us -> none  [the longest x1 67.9 us: on_device(): lax.all_gather(o_part, 'ctx', axis=0, tiled=True)]
    pallas_call x0 -> x3, Pallas kernels: none -> 202 us  [the longest x2 162 us: gather_pair(): pl.pallas_call(functools.partial(gather_kernel, devices, chunks), out_sha...]
    psum x2 -> x0, waiting for transfers between devices: 153 us -> none  [on_device(): lax.psum((query_down_gradient, key_value_down_gradient, query_up_gradient...]
    ppermute x8, waiting for transfers between devices: 110 us -> 43.2 us  [from_behind(): return lax.ppermute(shard, axis, pairs)]
    reduce_scatter x2, waiting for transfers between devices: 73.1 us -> 24.3 us  [the longest x1 24.3 us: on_device(): lax.psum_scatter(out_part.astype(jnp.bfloat16), 'tp', scatter_dimension=1...]
    all_gather x1, waiting for transfers between devices: 9.22 us -> 0.01 us  [on_device(): whole_tokens = lax.all_gather(tokens, 'tp', axis=1, tiled=True)]
    unnamed x128 -> x152, local copies, waits for them, and re-layouts: 19 us -> 12.9 us
  transfers between devices with their start and end apart: 18 -> 12, of which waited for: 17 -> 10; matrix products, arithmetic and copies ran while one was open for 11% -> 10% of each run, Pallas kernels for 0% -> 40%
where the time goes in v1:
time: 506 us; the launch traced here: 501 us
  Pallas kernels  202 us (40%)
  waiting for transfers between devices  92.8 us (18%)
  matrix products  70.6 us (14%)
  blocking collectives  35.3 us (7%)
  local copies, waits for them, and re-layouts  35 us (7%)
  other arithmetic  31.6 us (6%)
  starting transfers between devices  18.4 us (4%)
  between operations  15.2 us (3%)
    pallas_call x2, Pallas kernels, gather_pair(): pl.pallas_call(functools.partial(gather_kernel, devices, chunks), out_sha...  162 us
    ppermute x8, waiting for transfers between devices, from_behind(): return lax.ppermute(shard, axis, pairs)  43.2 us
    pallas_call x1, Pallas kernels, reduce_gradients(): pl.pallas_call(functools.partial(reduce_kernel, devices, sharers, split),...  40 us
    all_gather x1, waiting for transfers between devices, on_device(): output_gradient = lax.all_gather(grad_mine, 'tp', axis=1, tiled=True)  24.6 us
    reduce_scatter x1, waiting for transfers between devices, on_device(): lax.psum_scatter(out_part.astype(jnp.bfloat16), 'tp', scatter_dimension=1...  24.3 us
    ppermute x8, starting transfers between devices, from_behind(): return lax.ppermute(shard, axis, pairs)  18.1 us
    unnamed x152, local copies, waits for them, and re-layouts  12.9 us
    psum x1, blocking collectives, on_device(): output_lowrank = lax.psum(low_part, 'tp').astype(jnp.bfloat16)  11.2 us
  transfers between devices with their start and end apart: 12, of which 10 were waited for; matrix products, arithmetic and copies ran while one was open for 10% of the time, Pallas kernels for 40%

profile of v1, /device:TPU:12, one launch (start us, length us, event | category | flops | bytes accessed | tf_op | source)
XLA Modules:
  0.0 501.2 jit_solution(17295368850858359467)
XLA Ops:
  10.5 1.5 copy.102
  15.1 4.2 fusion.48
  19.3 56.3 %shard_map.268 = (bf16[8,672,256]{2,1,0:T(8,128)(2,1)}, bf16[8,672,256]{2,1,0:T(8,128)(2,1)}) custom-call(bf16[672,256]{1,0:T(8,128)(2,1)} %get-tuple-element.43.a_ref, bf16[672,256]{1,0:T(8,128)(2,1)} %get-tuple-element.42.b_ref), custom_call_target="tpu_custom_call" | custom-call | bytes 96337920 | tf_op jit(solution)/shard_map/pallas_call | solution.py:108
  75.6 5.8 %multiply_convert_fusion = (bf16[672,512]{1,0:T(8,128)(2,1)}, bf16[672,512]{1,0:T(8,128)(2,1)}) fusion(f32[672,512]{1,0:T(8,128)S(1)} %copy.103, s32[672,512]{1,0:T(8,128)} %param.33, f32[672,512]{1,0:T(8,128)S(1)} %copy-done.8, s32[672,512]{1,0:T(8,128)} %param.27), kind=kLoop, calls=%fused_computation.52 | loop fusion | flops 23396352 | bytes 6881280 | tf_op jit(solution)/shard_map/convert_element_type | solution.py:237
  82.2 105.9 %shard_map.269 = (bf16[8,672,512]{2,1,0:T(8,128)(2,1)}, bf16[8,672,512]{2,1,0:T(8,128)(2,1)}) custom-call(bf16[672,512]{1,0:T(8,128)(2,1)} %get-tuple-element.23.a_ref, bf16[672,512]{1,0:T(8,128)(2,1)} %get-tuple-element.24.b_ref), custom_call_target="tpu_custom_call" | custom-call | bytes 192675840 | tf_op jit(solution)/shard_map/pallas_call | solution.py:108
  188.2 1.6 fusion.34
  189.8 2.7 fusion.2
  193.0 2.3 fusion.4
  201.9 4.1 collective-permute-start
  206.0 1.9 collective-permute-start.1
  207.9 1.9 collective-permute-start.2
  209.8 2.2 collective-permute-start.3
  212.1 1.6 fusion.125
  218.8 1.9 collective-permute-done
  221.6 4.6 collective-permute-done.1
  227.3 4.6 collective-permute-done.2
  232.9 4.6 collective-permute-done.3
  239.3 5.6 %fusion.14 = f32[2,2,256,1280]{2,3,1,0:T(8,128)} fusion(bf16[1280,2,128,1]{0,2,3,1:T(8,128)(2,1)} %bitcast.299, pred[256,1280]{0,1:T(8,128)(4,1)} %fusion.34, bf16[256,2,2,64]{3,0,2,1:T(8,128)(2,1)} %bitcast.302, bf16[256,2,2,64]{3,0,2,1:T(8,128)(2,1)} %bitcast.304), kind=kOutput, calls=%fused_computation.28 | convolution fusion | flops 340003072 | bytes 6488064 | tf_op jit(solution)/shard_map/div | solution.py:292
  244.9 3.0 fusion.37
  248.0 5.8 %convolution_convert_fusion = bf16[256,5376]{0,1:T(8,128)(2,1)} fusion(bf16[5376,512]{1,0:T(8,128)(2,1)} %bitcast.266, bf16[256,512]{0,1:T(8,128)(2,1)S(1)} %bitcast.284), kind=kOutput, calls=%fused_computation.4 | convolution fusion | flops 1410662400 | bytes 8519680 | tf_op jit(solution)/shard_map/dot_general | solution.py:411
  254.8 11.2 %psum.49 = bf16[256,16]{0,1:T(8,128)(2,1)S(1)} all-reduce(f32[256,16]{0,1:T(8,128)S(1)} %fusion.133), channel_id=1, replica_groups=mesh['ctx'=8,'tp'=4] {'tp'}, use_global_device_ids=true, to_apply=%region_5.6 | all-reduce | flops 4096 | bytes 24576 | tf_op jit(solution)/shard_map/psum | solution.py:413
  266.0 24.3 %reduce-scatter.3.cloned.1.call-done = bf16[256,1344]{0,1:T(8,128)(2,1)} async-done(((bf16[256,5376]{0,1:T(8,128)(2,1)}), bf16[256,1344]{0,1:T(8,128)(2,1)}) %reduce-scatter.3.cloned.1.call-update) | async-done | bytes 688144 | tf_op jit(solution)/shard_map/reduce_scatter | solution.py:415
  290.3 3.1 fusion.22
  293.4 6.0 %all-reduce.1 = (f32[256,1]{0,1:T(1,128)S(1)}, f32[256,1]{0,1:T(1,128)S(1)}) all-reduce(f32[256,1]{0,1:T(1,128)S(1)} %bitcast.313, f32[256,1]{0,1:T(1,128)S(1)} %bitcast.312), channel_id=1, replica_groups=mesh['ctx'=8,'tp'=4] {'tp'}, use_global_device_ids=true, to_apply=%region_7.8 | all-reduce | flops 512 | bytes 4096 | tf_op jit(solution)/shard_map/psum | solution.py:418
  299.5 3.2 fusion.21
  304.9 24.6 %all-gather.5.cloned.1.call-done = bf16[256,5376]{0,1:T(8,128)(2,1)} async-done(((bf16[256,1344]{0,1:T(8,128)(2,1)}), bf16[256,5376]{0,1:T(8,128)(2,1)}) %all-gather.5.cloned.1.call-update) | async-done | bytes 2752528 | tf_op jit(solution)/shard_map/all_gather | solution.py:426
  329.5 5.1 %fusion.126 = f32[256,512]{1,0:T(8,128)S(1)} fusion(bf16[256,5376]{0,1:T(8,128)(2,1)} %all-gather.5.cloned.1.call-done, bf16[5376,512]{1,0:T(8,128)(2,1)} %bitcast.267), kind=kOutput, calls=%fused_computation.226 | convolution fusion | flops 1409286144 | bytes 8781824 | tf_op jit(solution)/shard_map/dot_general | solution.py:435
  337.2 3.2 fusion.127
  340.5 9.5 %fusion.17 = f32[2,128,2,256]{3,1,2,0:T(8,128)} fusion(bf16[1280,2,128,1]{0,2,3,1:T(8,128)(2,1)} %bitcast.300, f32[2,2,256,1280]{2,3,1,0:T(8,128)} %fusion.14, f32[2,1280,256,2]{2,1,3,0:T(8,128)} %fusion.127), kind=kOutput, calls=%fused_computation.35 | convolution fusion | flops 342100224 | bytes 11665408 | tf_op jit(solution)/shard_map/kgtl,lkd->tkgd/dot_general | solution.py:317
  350.0 9.8 %fusion.16 = f32[2,128,1280,1]{2,1,3,0:T(8,128)} fusion(f32[2,2,256,1280]{2,3,1,0:T(8,128)} %fusion.14, f32[2,1280,256,2]{2,1,3,0:T(8,128)} %fusion.127, bf16[256,2,2,64]{3,0,2,1:T(8,128)(2,1)S(1)} %bitcast.303, bf16[256,2,2,64]{3,0,2,1:T(8,128)(2,1)S(1)} %bitcast.305), kind=kOutput, calls=%fused_computation.34 | convolution fusion | flops 342624512 | bytes 12058624 | tf_op jit(solution)/shard_map/kgtl,tkgd->lkd/dot_general | solution.py:320
  359.7 3.6 fusion.29
  364.2 2.0 copy.148
  366.2 1.9 copy.147
  368.1 1.6 multiply_add_fusion
  370.5 1.7 fusion.12
  373.7 2.4 collective-permute-start.6
  376.2 1.9 collective-permute-start.5
  378.1 2.2 collective-permute-start.4
  381.7 1.6 fusion.128
  384.5 5.6 %collective-permute-done.6 = bf16[2,256,256]{1,2,0:T(8,128)(2,1)S(1)} collective-permute-done((bf16[2,256,256]{1,2,0:T(8,128)(2,1)S(1)}, bf16[2,256,256]{1,2,0:T(8,128)(2,1)S(1)}, u32[]{:S(2)}, u32[]{:S(2)}) %collective-permute-start.6) | collective-permute-done | bytes 262176 | tf_op jit(solution)/shard_map/ppermute | solution.py:44
  390.1 9.6 %collective-permute-done.5 = bf16[2,256,256]{1,2,0:T(8,128)(2,1)S(1)} collective-permute-done((bf16[2,256,256]{1,2,0:T(8,128)(2,1)S(1)}, bf16[2,256,256]{1,2,0:T(8,128)(2,1)S(1)}, u32[]{:S(2)}, u32[]{:S(2)}) %collective-permute-start.5) | collective-permute-done | bytes 262176 | tf_op jit(solution)/shard_map/ppermute | solution.py:44
  399.7 11.2 %collective-permute-done.4 = bf16[2,256,256]{1,2,0:T(8,128)(2,1)S(1)} collective-permute-done((bf16[2,256,256]{1,2,0:T(8,128)(2,1)S(1)}, bf16[2,256,256]{1,2,0:T(8,128)(2,1)S(1)}, u32[]{:S(2)}, u32[]{:S(2)}) %collective-permute-start.4) | collective-permute-done | bytes 262176 | tf_op jit(solution)/shard_map/ppermute | solution.py:44
  414.4 2.4 fusion.1
  420.1 10.6 %all-reduce = (bf16[256,16]{0,1:T(8,128)(2,1)S(1)}, bf16[256,16]{0,1:T(8,128)(2,1)S(1)}, bf16[256,16]{0,1:T(8,128)(2,1)S(1)}) all-reduce(f32[256,16]{0,1:T(8,128)S(1)} %fusion.129, f32[256,16]{0,1:T(8,128)S(1)} %fusion.83, f32[256,16]{0,1:T(8,128)S(1)} %fusion.80), channel_id=1, replica_groups=mesh['ctx'=8,'tp'=4] {'tp'}, use_global_device_ids=true, to_apply=%region_14.15 | all-reduce | flops 12288 | bytes 73728 | tf_op jit(solution)/shard_map/psum | solution.py:481
  432.0 40.0 %shard_map.270 = (f32[4,8,8,1408]{3,2,1,0:T(8,128)}, f32[8,8,384]{2,1,0:T(8,128)}) custom-call(f32[64,1792]{1,0:T(8,128)} %concatenate.50.g_ref), custom_call_target="tpu_custom_call" | custom-call | tf_op jit(solution)/shard_map/pallas_call | solution.py:206
  480.9 1.6 convolution_add_fusion.3
  482.5 2.4 fusion.26
  484.9 7.5 %psum.55 = f32[256,1]{0,1:T(1,128)S(1)} all-reduce(f32[256,1]{0,1:T(1,128)S(1)} %bitcast.310), channel_id=1, replica_groups=mesh['ctx'=8,'tp'=4] {'tp'}, use_global_device_ids=true, to_apply=%region_18.19 | all-reduce | flops 256 | bytes 2048 | tf_op jit(solution)/shard_map/psum | solution.py:502
  (263 shorter events, 54.0 us)
Async XLA Ops:
  7.2 283.2 %copy-start = (bf16[16,5376]{1,0:T(8,128)(2,1)S(1)}, bf16[16,5376]{1,0:T(8,128)(2,1)}, u32[]{:S(2)}) copy-start(bf16[16,5376]{1,0:T(8,128)(2,1)} %param.41) | copy-start | bytes 516100
  7.2 182.6 %all-gather.3.cloned.1.call-start = ((), (), s32[]{:S(2)}) async-start(), calls=%async_computation.2 | async-start | bytes 3440640 | tf_op jit(solution)/shard_map/all_gather | solution.py:368
  7.9 282.4 %reduce-scatter.3.cloned.1.call-start = ((), (), s32[]{:S(2)}) async-start(), calls=%async_computation.3 | async-start | bytes 3440640 | tf_op jit(solution)/shard_map/reduce_scatter | solution.py:415
  15.1 60.5 %copy-start.8 = (f32[672,512]{1,0:T(8,128)S(1)}, f32[672,512]{1,0:T(8,128)}, u32[]{:S(2)}) copy-start(f32[672,512]{1,0:T(8,128)} %copy.102) | copy-start | bytes 4128772
  82.0 134.8 %copy-start.16 = (f32[256,64]{1,0:T(8,128)}, f32[256,64]{1,0:T(8,128)S(1)}, u32[]{:S(2)}) copy-start(f32[256,64]{1,0:T(8,128)S(1)} %get-tuple-element.72) | copy-start | bytes 196612
  82.0 134.8 %copy-start.18 = (f32[256,64]{1,0:T(8,128)}, f32[256,64]{1,0:T(8,128)S(1)}, u32[]{:S(2)}) copy-start(f32[256,64]{1,0:T(8,128)S(1)} %get-tuple-element.73) | copy-start | bytes 196612
  82.2 119.0 %copy-start.23 = (f32[256,64]{0,1:T(8,128)}, f32[256,64]{0,1:T(8,128)S(1)}, u32[]{:S(2)}) copy-start(f32[256,64]{0,1:T(8,128)S(1)} %copy.106) | copy-start | bytes 196612
  188.1 4.9 copy-start.42
  195.8 4.7 copy-start.35
  197.1 14.9 %slice-start = ((s8[5505024]{0:T(1024)(128)(4,1)}), s8[4194304]{0:T(1024)(128)(4,1)S(1)}, s32[]{:S(2)}) async-start(s8[5505024]{0:T(1024)(128)(4,1)} %bitcast.260), calls=%async_computation.6 | async-start | bytes 8388608
  198.4 13.7 %slice-start.1 = ((s8[5505024]{0:T(1024)(128)(4,1)}), s8[1310720]{0:T(1024)(128)(4,1)S(1)}, s32[]{:S(2)}) async-start(s8[5505024]{0:T(1024)(128)(4,1)} %bitcast.260), calls=%async_computation.7 | async-start | bytes 2621440
  201.9 18.8 %collective-permute-start = (bf16[2,256,256]{1,2,0:T(8,128)(2,1)}, bf16[2,256,256]{1,2,0:T(8,128)(2,1)}, u32[]{:S(2)}, u32[]{:S(2)}) collective-permute-start(bf16[2,256,256]{1,2,0:T(8,128)(2,1)} %pad_maximum_fusion.2), channel_id=1, source_target_pairs={{0,16},{4,20},{8,24},{12,28},{1,17},{5,21},{9,25},{13,29},{2,18},{... | collective-permute-start | bytes 786440 | tf_op jit(solution)/shard_map/ppermute | solution.py:44
  206.0 20.3 %collective-permute-start.1 = (bf16[2,256,256]{1,2,0:T(8,128)(2,1)}, bf16[2,256,256]{1,2,0:T(8,128)(2,1)}, u32[]{:S(2)}, u32[]{:S(2)}) collective-permute-start(bf16[2,256,256]{1,2,0:T(8,128)(2,1)} %pad_maximum_fusion.2), channel_id=1, source_target_pairs={{0,12},{4,16},{8,20},{12,24},{16,28},{1,13},{5,17},{9,21},{13,25},... | collective-permute-start | bytes 786440 | tf_op jit(solution)/shard_map/ppermute | solution.py:44
  207.9 24.0 %collective-permute-start.2 = (bf16[2,256,256]{1,2,0:T(8,128)(2,1)}, bf16[2,256,256]{1,2,0:T(8,128)(2,1)}, u32[]{:S(2)}, u32[]{:S(2)}) collective-permute-start(bf16[2,256,256]{1,2,0:T(8,128)(2,1)} %pad_maximum_fusion.2), channel_id=1, source_target_pairs={{0,8},{4,12},{8,16},{12,20},{16,24},{20,28},{1,9},{5,13},{9,17},{1... | collective-permute-start | bytes 786440 | tf_op jit(solution)/shard_map/ppermute | solution.py:44
  209.8 27.6 %collective-permute-start.3 = (bf16[2,256,256]{1,2,0:T(8,128)(2,1)}, bf16[2,256,256]{1,2,0:T(8,128)(2,1)}, u32[]{:S(2)}, u32[]{:S(2)}) collective-permute-start(bf16[2,256,256]{1,2,0:T(8,128)(2,1)} %pad_maximum_fusion.2), channel_id=1, source_target_pairs={{0,4},{4,8},{8,12},{12,16},{16,20},{20,24},{24,28},{1,5},{5,9},{9,... | collective-permute-start | bytes 786440 | tf_op jit(solution)/shard_map/ppermute | solution.py:44
  248.0 6.7 %copy-start.13 = (bf16[2,128,2,256]{3,1,2,0:T(8,128)(2,1)}, bf16[2,128,2,256]{3,1,2,0:T(8,128)(2,1)S(1)}, u32[]{:S(2)}) copy-start(bf16[2,128,2,256]{3,1,2,0:T(8,128)(2,1)S(1)} %fusion.37) | copy-start | bytes 786436
  253.9 75.7 %all-gather.5.cloned.1.call-start = ((), (), s32[]{:S(2)}) async-start(), calls=%async_computation.4 | async-start | bytes 3440640 | tf_op jit(solution)/shard_map/all_gather | solution.py:426
  266.0 27.4 %copy-start.43 = (bf16[256,16]{0,1:T(8,128)(2,1)}, bf16[256,16]{0,1:T(8,128)(2,1)S(1)}, u32[]{:S(2)}) copy-start(bf16[256,16]{0,1:T(8,128)(2,1)S(1)} %psum.49) | copy-start | bytes 24580
  266.0 33.4 %copy-start.4 = (bf16[256,1344]{0,1:T(8,128)(2,1)S(1)}, bf16[256,1344]{0,1:T(8,128)(2,1)}, u32[]{:S(2)}) copy-start(bf16[256,1344]{0,1:T(8,128)(2,1)} %param.21) | copy-start | bytes 2064388
  299.4 3.5 copy-start.61
  299.4 4.1 copy-start.56
  299.5 4.7 copy-start.49
  302.7 179.8 %reduce-scatter.5.cloned.1.call-start = ((), (), s32[]{:S(2)}) async-start(), calls=%async_computation.5 | async-start | bytes 3440640 | tf_op jit(solution)/shard_map/reduce_scatter | solution.py:487
  329.5 5.1 %copy-start.2 = (bf16[256,5376]{0,1:T(8,128)(2,1)S(1)}, bf16[256,5376]{0,1:T(8,128)(2,1)}, u32[]{:S(2)}) copy-start(bf16[256,5376]{0,1:T(8,128)(2,1)} %all-gather.5.cloned.1.call-done) | copy-start | bytes 8257540
  335.1 5.4 %copy-start.33 = (bf16[256,16]{0,1:T(8,128)(2,1)}, bf16[256,16]{0,1:T(8,128)(2,1)S(1)}, u32[]{:S(2)}) copy-start(bf16[256,16]{0,1:T(8,128)(2,1)S(1)} %convolution_convert_fusion.1) | copy-start | bytes 24580
  340.5 9.5 %copy-start.28 = (bf16[256,4,64]{2,0,1:T(8,128)(2,1)S(1)}, bf16[256,4,64]{2,0,1:T(8,128)(2,1)}, u32[]{:S(2)}) copy-start(bf16[256,4,64]{2,0,1:T(8,128)(2,1)} %copy.113) | copy-start | bytes 393220
  340.5 9.5 %copy-start.29 = (bf16[256,4,64]{2,0,1:T(8,128)(2,1)S(1)}, bf16[256,4,64]{2,0,1:T(8,128)(2,1)}, u32[]{:S(2)}) copy-start(bf16[256,4,64]{2,0,1:T(8,128)(2,1)} %copy.112) | copy-start | bytes 393220
  359.7 3.6 copy-start.26
  363.4 4.8 copy-start.17
  363.4 6.4 %copy-start.57 = (f32[128]{0:T(128)S(1)}, f32[128]{0:T(128)}, u32[]{:S(2)}) copy-start(f32[128]{0:T(128)} %param.24) | copy-start | bytes 1540
  368.1 13.5 %slice-start.2 = ((s8[5505024]{0:T(1024)(128)(4,1)}), s8[4194304]{0:T(1024)(128)(4,1)S(1)}, s32[]{:S(2)}) async-start(s8[5505024]{0:T(1024)(128)(4,1)} %bitcast.263), calls=%async_computation.8 | async-start | bytes 8388608
  370.5 11.1 %slice-start.3 = ((s8[5505024]{0:T(1024)(128)(4,1)}), s8[1310720]{0:T(1024)(128)(4,1)S(1)}, s32[]{:S(2)}) async-start(s8[5505024]{0:T(1024)(128)(4,1)} %bitcast.263), calls=%async_computation.9 | async-start | bytes 2621440
  372.2 8.4 %copy-start.25 = (f32[256,4]{1,0:T(8,128)S(1)}, f32[256,4]{1,0:T(8,128)}, u32[]{:S(2)}) copy-start(f32[256,4]{1,0:T(8,128)} %copy.121) | copy-start | bytes 12292
  372.2 8.8 %copy-start.22 = (f32[256,4]{1,0:T(8,128)S(1)}, f32[256,4]{1,0:T(8,128)}, u32[]{:S(2)}) copy-start(f32[256,4]{1,0:T(8,128)} %copy-done.21) | copy-start | bytes 12292
  372.3 9.0 %copy-start.53 = (f32[512]{0:T(512)S(1)}, f32[512]{0:T(512)}, u32[]{:S(2)}) copy-start(f32[512]{0:T(512)} %broadcast_bitcast_fusion) | copy-start | bytes 6148
  372.3 12.1 %collective-permute-start.7 = (bf16[2,256,256]{1,2,0:T(8,128)(2,1)S(1)}, bf16[2,256,256]{1,2,0:T(8,128)(2,1)S(1)}, u32[]{:S(2)}, u32[]{:S(2)}) collective-permute-start(bf16[2,256,256]{1,2,0:T(8,128)(2,1)S(1)} %get-tuple-element.45), channel_id=1, source_target_pairs={{16,0},{20,4},{24,8},{28,12},{17,1},{21,5},{25,9},{29,13},{18,2},{... | collective-permute-start | bytes 786440 | tf_op jit(solution)/shard_map/ppermute | solution.py:44
  373.7 16.3 %collective-permute-start.6 = (bf16[2,256,256]{1,2,0:T(8,128)(2,1)S(1)}, bf16[2,256,256]{1,2,0:T(8,128)(2,1)S(1)}, u32[]{:S(2)}, u32[]{:S(2)}) collective-permute-start(bf16[2,256,256]{1,2,0:T(8,128)(2,1)S(1)} %get-tuple-element.46), channel_id=1, source_target_pairs={{12,0},{16,4},{20,8},{24,12},{28,16},{13,1},{17,5},{21,9},{25,13},... | collective-permute-start | bytes 786440 | tf_op jit(solution)/shard_map/ppermute | solution.py:44
  376.2 23.5 %collective-permute-start.5 = (bf16[2,256,256]{1,2,0:T(8,128)(2,1)S(1)}, bf16[2,256,256]{1,2,0:T(8,128)(2,1)S(1)}, u32[]{:S(2)}, u32[]{:S(2)}) collective-permute-start(bf16[2,256,256]{1,2,0:T(8,128)(2,1)S(1)} %get-tuple-element.47), channel_id=1, source_target_pairs={{8,0},{12,4},{16,8},{20,12},{24,16},{28,20},{9,1},{13,5},{17,9},{2... | collective-permute-start | bytes 786440 | tf_op jit(solution)/shard_map/ppermute | solution.py:44
  378.1 32.8 %collective-permute-start.4 = (bf16[2,256,256]{1,2,0:T(8,128)(2,1)S(1)}, bf16[2,256,256]{1,2,0:T(8,128)(2,1)S(1)}, u32[]{:S(2)}, u32[]{:S(2)}) collective-permute-start(bf16[2,256,256]{1,2,0:T(8,128)(2,1)S(1)} %get-tuple-element.44), channel_id=1, source_target_pairs={{4,0},{8,4},{12,8},{16,12},{20,16},{24,20},{28,24},{5,1},{9,5},{13... | collective-permute-start | bytes 786440 | tf_op jit(solution)/shard_map/ppermute | solution.py:44
  381.7 29.2 %copy-start.9 = (f32[2,128,1280,1]{2,1,3,0:T(8,128)S(1)}, f32[2,128,1280,1]{2,1,3,0:T(8,128)}, u32[]{:S(2)}) copy-start(f32[2,128,1280,1]{2,1,3,0:T(8,128)} %fusion.16) | copy-start | bytes 3932164
  383.3 27.8 %copy-start.24 = (f32[256,64]{0,1:T(8,128)S(1)}, f32[256,64]{0,1:T(8,128)}, u32[]{:S(2)}) copy-start(f32[256,64]{0,1:T(8,128)} %copy-done.23) | copy-start | bytes 196612
  383.3 27.8 %copy-start.62 = (f32[128]{0:T(128)S(1)}, f32[128]{0:T(128)}, u32[]{:S(2)}) copy-start(f32[128]{0:T(128)} %param.25) | copy-start | bytes 1540
  417.8 12.9 %copy-start.45 = (f32[1344]{0:T(1024)}, f32[1344]{0:T(1024)S(1)}, u32[]{:S(2)}) copy-start(f32[1344]{0:T(1024)S(1)} %dynamic_slice.29) | copy-start | bytes 16132
  418.5 12.2 %copy-start.51 = (f32[256]{0:T(256)S(1)}, f32[256]{0:T(256)}, u32[]{:S(2)}) copy-start(f32[256]{0:T(256)} %copy-done.50) | copy-start | bytes 3076
  482.4 10.0 %copy-start.58 = (f32[256]{0:T(256)S(1)}, f32[256]{0:T(256)}, u32[]{:S(2)}) copy-start(f32[256]{0:T(256)} %get-tuple-element.76) | copy-start | bytes 3076
  482.4 10.6 %copy-start.12 = (bf16[256,1344]{0,1:T(8,128)(2,1)S(1)}, bf16[256,1344]{0,1:T(8,128)(2,1)}, u32[]{:S(2)}) copy-start(bf16[256,1344]{0,1:T(8,128)(2,1)} %param.22) | copy-start | bytes 2064388
  482.5 10.6 %copy-start.52 = (f32[256]{0:T(256)S(1)}, f32[256]{0:T(256)}, u32[]{:S(2)}) copy-start(f32[256]{0:T(256)} %copy-done.50) | copy-start | bytes 3076
  482.5 10.6 %copy-start.59 = (f32[256]{0:T(256)S(1)}, f32[256]{0:T(256)}, u32[]{:S(2)}) copy-start(f32[256]{0:T(256)} %get-tuple-element.77) | copy-start | bytes 3076
  (36 other events, 59.0 us)
Sparse Core Ops, SparseCore 0:
  9.6 27.3 all-gather.2
  254.0 36.3 reduce-scatter.2
  302.8 26.6 all-gather.4
  417.0 33.4 reduce-scatter.4

commit v2 on v1

--- a/solution.py
+++ b/solution.py
@@ -223,6 +223,115 @@
     return down.reshape(sharers, height, split)[:, :, :width], up.reshape(up_shape)
 
 
+def share_kernel(chunks, parts_ref, small_ref, out_ref, small_out, *scratch):
+    core_in, staged, cross_in, small_in, core_sems, cross_sems, small_sems = scratch
+    side = lax.axis_index("tp")
+    chip, core = side // 2, side % 2
+    partner = chip * 2 + 1 - core
+    across = (1 - chip) * 2 + core
+    barrier = pltpu.get_barrier_semaphore()
+    for k in range(1, 4):
+        pl.semaphore_signal(barrier, inc=1, device_id={"tp": (side + k) % 4}, device_id_type=MESH)
+    pl.semaphore_wait(barrier, 3)
+    rows = parts_ref.shape[1] // chunks
+
+    def core_copy(far, chunk):
+        chip_to = far * (1 - chip) + (1 - far) * chip
+        part = pl.ds(chunk * rows, rows)
+        return pltpu.make_async_remote_copy(
+            src_ref=parts_ref.at[chip_to * 2 + 1 - core, part],
+            dst_ref=core_in.at[far, part],
+            send_sem=core_sems.at[0, far, chunk],
+            recv_sem=core_sems.at[1, far, chunk],
+            device_id={"tp": partner},
+            device_id_type=MESH,
+        )
+
+    to_core = {}
+    for far in (1, 0):
+        for chunk in range(chunks):
+            to_core[far, chunk] = core_copy(far, chunk)
+            to_core[far, chunk].start()
+    to_all = []
+    for k in range(1, 4):
+        copy = pltpu.make_async_remote_copy(
+            src_ref=small_ref,
+            dst_ref=small_in.at[side],
+            send_sem=small_sems.at[0, k],
+            recv_sem=small_sems.at[1, k],
+            device_id={"tp": (side + k) % 4},
+            device_id_type=MESH,
+        )
+        copy.start()
+        to_all.append(copy)
+    small_in[side] = small_ref[...]
+    to_across = []
+    for chunk in range(chunks):
+        part = pl.ds(chunk * rows, rows)
+        to_core[1, chunk].wait_recv()
+        staged[part, :] = (
+            parts_ref[across, part, :].astype(jnp.float32)
+            + core_in[1, part, :].astype(jnp.float32)
+        ).astype(jnp.bfloat16)
+        copy = pltpu.make_async_remote_copy(
+            src_ref=staged.at[part],
+            dst_ref=cross_in.at[part],
+            send_sem=cross_sems.at[0, chunk],
+            recv_sem=cross_sems.at[1, chunk],
+            device_id={"tp": across},
+            device_id_type=MESH,
+        )
+        copy.start()
+        to_across.append(copy)
+    for chunk in range(chunks):
+        part = pl.ds(chunk * rows, rows)
+        to_core[0, chunk].wait_recv()
+        out_ref[part, :] = parts_ref[side, part, :].astype(jnp.float32) + core_in[
+            0, part, :
+        ].astype(jnp.float32)
+    for copy in to_all:
+        copy.wait_recv()
+    small_out[...] = (small_in[0] + small_in[1]) + (small_in[2] + small_in[3])
+    for chunk in range(chunks):
+        part = pl.ds(chunk * rows, rows)
+        to_across[chunk].wait_recv()
+        out_ref[part, :] = out_ref[part, :] + cross_in[part, :].astype(jnp.float32)
+    for copy in list(to_core.values()) + to_all + to_across:
+        copy.wait_send()
+
+
+def share_sums(parts, small, collective_id):
+    sharers = lax.axis_size("tp")
+    _, count, share = parts.shape
+    if sharers != 4 or count % 64:
+        mine = lax.psum_scatter(parts, "tp", scatter_dimension=0, tiled=False)
+        return mine.astype(jnp.float32), lax.psum(small, "tp")
+    width = small.shape[1]
+    lanes = -(-width // 128) * 128
+    small = jnp.pad(small, ((0, 0), (0, lanes - width)))
+    chunks = 4
+    mine, small = pl.pallas_call(
+        functools.partial(share_kernel, chunks),
+        out_shape=[
+            jax.ShapeDtypeStruct((count, share), jnp.float32),
+            jax.ShapeDtypeStruct((count, lanes), jnp.float32),
+        ],
+        in_specs=[pl.BlockSpec(memory_space=pltpu.VMEM)] * 2,
+        out_specs=[pl.BlockSpec(memory_space=pltpu.VMEM)] * 2,
+        scratch_shapes=[
+            pltpu.VMEM((2, count, share), jnp.bfloat16),
+            pltpu.VMEM((count, share), jnp.bfloat16),
+            pltpu.VMEM((count, share), jnp.bfloat16),
+            pltpu.VMEM((sharers, count, lanes), jnp.float32),
+            pltpu.SemaphoreType.DMA((2, 2, chunks)),
+            pltpu.SemaphoreType.DMA((2, chunks)),
+            pltpu.SemaphoreType.DMA((2, sharers)),
+        ],
+        compiler_params=pltpu.CompilerParams(collective_id=collective_id, has_side_effects=True),
+    )(parts, small)
+    return mine, small[:, :width]
+
+
 def dequantize(codes, scodes, second, row_start):
     height, width = codes.shape
     levels = jnp.zeros(codes.shape, jnp.float32)
@@ -361,10 +470,6 @@
     v_part = dequantize(kv_codes[1], kv_scodes[1], kv_second[1], row_start)
     o_part = dequantize(o_codes, o_scodes, o_second, row_start)
     key_matrix, value_matrix = gather_pair(k_part, v_part, 1)
-    q_part, o_part, key_matrix, value_matrix = lax.optimization_barrier(
-        (q_part, o_part, key_matrix, value_matrix)
-    )
-    query_matrix, output_matrix = gather_pair(q_part, o_part, 2)
     whole_tokens = lax.all_gather(tokens, "tp", axis=1, tiled=True)
     wide = whole_tokens.astype(jnp.float32)
     row_scale = lax.rsqrt(jnp.mean(wide * wide, axis=1, keepdims=True) + EPSILON)
@@ -378,9 +483,6 @@
     value_lowrank = jnp.dot(
         normalized_input, kv_down[1], preferred_element_type=jnp.float32
     ).astype(jnp.bfloat16)
-    query_rows = jnp.dot(
-        normalized_input, query_matrix, preferred_element_type=jnp.float32
-    ) + ADAPTER_SCALE * jnp.dot(query_lowrank, query_up, preferred_element_type=jnp.float32)
     key = jnp.dot(
         normalized_input, key_matrix, preferred_element_type=jnp.float32
     ) + ADAPTER_SCALE * jnp.dot(key_lowrank, key_value_up[0], preferred_element_type=jnp.float32)
@@ -391,30 +493,44 @@
     query_pos = ctx_rank * count + jnp.arange(count, dtype=jnp.int32)
     key_pos = ctx_rank * count - WINDOW_TOKENS + jnp.arange(WINDOW_TOKENS + count, dtype=jnp.int32)
     cosine, sine = rope_tables(query_pos)
-    q_heads = query_rows.reshape(count, q_heads_here, HEAD_SIZE)
-    q_normed, q_scale = head_norm(q_heads, query_gain)
-    q_rot = rotate(q_normed, cosine, sine).astype(jnp.bfloat16)
     key_head_rows = key.reshape(count, kv_heads_here, HEAD_SIZE)
     k_normed, k_scale = head_norm(key_head_rows, key_gain)
     k_rot = rotate(k_normed, cosine, sine).astype(jnp.bfloat16)
     piece_rows = min(WINDOW_TOKENS, count)
     pieces = WINDOW_TOKENS // piece_rows
     stacked = jnp.stack([k_rot.reshape(count, kv_width), value_rows])
+    q_part, o_part, stacked = lax.optimization_barrier((q_part, o_part, stacked))
     arrived = []
     for offset in range(pieces, 0, -1):
         arrived.append(from_behind(stacked, "ctx", offset))
+    query_matrix, output_matrix = gather_pair(q_part, o_part, 2)
+    query_rows = jnp.dot(
+        normalized_input, query_matrix, preferred_element_type=jnp.float32
+    ) + ADAPTER_SCALE * jnp.dot(query_lowrank, query_up, preferred_element_type=jnp.float32)
+    q_heads = query_rows.reshape(count, q_heads_here, HEAD_SIZE)
+    q_normed, q_scale = head_norm(q_heads, query_gain)
+    q_rot = rotate(q_normed, cosine, sine).astype(jnp.bfloat16)
     window = jnp.concatenate(arrived + [stacked], axis=1)
     window_keys = window[0].reshape(WINDOW_TOKENS + count, kv_heads_here, HEAD_SIZE)
     window_values = window[1].reshape(WINDOW_TOKENS + count, kv_heads_here, HEAD_SIZE)
     attended_rows = attention_forward(q_rot, window_keys, window_values, query_pos, key_pos)
     low_part = jnp.dot(attended_rows, output_down, preferred_element_type=jnp.float32)
-    out_part = jnp.dot(attended_rows, output_matrix.T, preferred_element_type=jnp.float32)
+    sharers = lax.axis_size("tp")
+    out_part = jnp.stack(
+        [
+            jnp.dot(
+                attended_rows,
+                output_matrix[k * share : (k + 1) * share].T,
+                preferred_element_type=jnp.float32,
+            ).astype(jnp.bfloat16)
+            for k in range(sharers)
+        ]
+    )
+    out_mine, low_sum = share_sums(out_part, low_part, 4)
     gain_mine = lax.dynamic_slice_in_dim(post_gain, column_start, share, 0)
-    output_lowrank = lax.psum(low_part, "tp").astype(jnp.bfloat16)
+    output_lowrank = low_sum.astype(jnp.bfloat16)
     up_mine = lax.dynamic_slice_in_dim(output_up, column_start, share, 1)
-    out_mine = lax.psum_scatter(
-        out_part.astype(jnp.bfloat16), "tp", scatter_dimension=1, tiled=True
-    ).astype(jnp.float32) + ADAPTER_SCALE * jnp.dot(output_lowrank, up_mine, preferred_element_type=jnp.float32)
+    out_mine = out_mine + ADAPTER_SCALE * jnp.dot(output_lowrank, up_mine, preferred_element_type=jnp.float32)
     square_sum = lax.psum(jnp.sum(out_mine * out_mine, axis=1, keepdims=True), "tp")
     out_scale = lax.rsqrt(square_sum / D + EPSILON)
     mixed = (tokens.astype(jnp.float32) + out_mine * out_scale * gain_mine).astype(jnp.bfloat16)
@@ -471,22 +587,28 @@
     value_mixture = jnp.dot(
         value_gradient_lowrank, key_value_up[1].T, preferred_element_type=jnp.float32
     )
-    into_part = jnp.dot(query_gradient_lowrank, query_matrix.T, preferred_element_type=jnp.float32)
-    into_part = into_part + jnp.dot(
-        key_gradient_lowrank, key_matrix.T, preferred_element_type=jnp.float32
-    )
-    into_part = into_part + jnp.dot(
-        value_gradient_lowrank, value_matrix.T, preferred_element_type=jnp.float32
-    )
-    query_mixture, key_mixture, value_mixture = lax.psum(
-        (query_mixture, key_mixture, value_mixture), "tp"
-    )
+    into_parts = []
+    for k in range(sharers):
+        rows = slice(k * share, (k + 1) * share)
+        into_part = jnp.dot(
+            query_gradient_lowrank, query_matrix[rows].T, preferred_element_type=jnp.float32
+        )
+        into_part = into_part + jnp.dot(
+            key_gradient_lowrank, key_matrix[rows].T, preferred_element_type=jnp.float32
+        )
+        into_part = into_part + jnp.dot(
+            value_gradient_lowrank, value_matrix[rows].T, preferred_element_type=jnp.float32
+        )
+        into_parts.append(into_part.astype(jnp.bfloat16))
+    into_mine, mixture_sum = share_sums(
+        jnp.stack(into_parts),
+        jnp.concatenate([query_mixture, key_mixture, value_mixture], axis=1),
+        5,
+    )
+    query_mixture, key_mixture, value_mixture = jnp.split(mixture_sum, 3, axis=1)
     query_mixture = query_mixture.astype(jnp.bfloat16)
     key_mixture = key_mixture.astype(jnp.bfloat16)
     value_mixture = value_mixture.astype(jnp.bfloat16)
-    into_mine = lax.psum_scatter(
-        into_part.astype(jnp.bfloat16), "tp", scatter_dimension=1, tiled=True
-    ).astype(jnp.float32)
     q_down_mine = lax.dynamic_slice_in_dim(q_down, column_start, share, 0)
     k_down_mine = lax.dynamic_slice_in_dim(kv_down[0], column_start, share, 0)
     v_down_mine = lax.dynamic_slice_in_dim(kv_down[1], column_start, share, 0)
@@ -520,7 +642,6 @@
     )
     down_sum, up_sum = reduce_gradients(ADAPTER_SCALE * down_part, ADAPTER_SCALE * up_part, 3)
     rank = query_up.shape[0]
-    sharers = down_sum.shape[0]
     down_sum = down_sum.reshape(sharers, 4, rank, share)
     down_turned = down_sum[:, :3].transpose(1, 0, 3, 2).reshape(3, sharers * share, rank)
     query_down_gradient = down_turned[0]

time: 506 us -> 567 us (1.12)
  Pallas kernels: 202 us -> 296 us
  waiting for transfers between devices: 92.8 us -> 11 us
  local copies, waits for them, and re-layouts: 35 us -> 78.5 us
  blocking collectives: 35.3 us -> 14.2 us
  matrix products: 70.6 us -> 88.5 us
  other arithmetic: 31.6 us -> 38.2 us
    pallas_call x0 -> x2, Pallas kernels: none -> 54.8 us  [share_sums(): pl.pallas_call(functools.partial(share_kernel, chunks), out_shape=[jax.Sh...]
    ppermute x8, waiting for transfers between devices: 43.2 us -> 0.03 us  [from_behind(): return lax.ppermute(shard, axis, pairs)]
    pallas_call x2, Pallas kernels: 162 us -> 187 us  [gather_pair(): pl.pallas_call(functools.partial(gather_kernel, devices, chunks), out_sha...]
    reduce_scatter x2 -> x0, waiting for transfers between devices: 24.3 us -> none  [the longest x1 24.3 us: on_device(): lax.psum_scatter(out_part.astype(jnp.bfloat16), 'tp', scatter_dimension=1...]
    psum x2 -> x0, blocking collectives: 21.8 us -> none  [the longest x1 11.2 us: on_device(): output_lowrank = lax.psum(low_part, 'tp').astype(jnp.bfloat16)]
    slice x0 -> x3, local copies, waits for them, and re-layouts: none -> 15.6 us  [the longest x1 5.7 us: on_device(): query_matrix[rows]]
    all_gather x1, waiting for transfers between devices: 24.6 us -> 10.3 us  [on_device(): output_gradient = lax.all_gather(grad_mine, 'tp', axis=1, tiled=True)]
    pallas_call x1, Pallas kernels: 40 us -> 54.2 us  [reduce_gradients(): pl.pallas_call(functools.partial(reduce_kernel, devices, sharers, split),...]
  transfers between devices with their start and end apart: 12 -> 10, of which waited for: 10 -> 1; matrix products, arithmetic and copies ran while one was open for 10% -> 13% of each run, Pallas kernels for 40% -> 33%
where the time goes in v2:
time: 567 us; the launch traced here: 560 us
  Pallas kernels  296 us (52%)
  matrix products  88.5 us (16%)
  local copies, waits for them, and re-layouts  78.5 us (14%)
  other arithmetic  38.2 us (7%)
  starting transfers between devices  18.7 us (3%)
  between operations  15.5 us (3%)
  blocking collectives  14.2 us (3%)
  waiting for transfers between devices  11 us (2%)
    pallas_call x2, Pallas kernels, gather_pair(): pl.pallas_call(functools.partial(gather_kernel, devices, chunks), out_sha...  187 us
    pallas_call x2, Pallas kernels, share_sums(): pl.pallas_call(functools.partial(share_kernel, chunks), out_shape=[jax.Sh...  54.8 us
    pallas_call x1, Pallas kernels, reduce_gradients(): pl.pallas_call(functools.partial(reduce_kernel, devices, sharers, split),...  54.2 us
    unnamed x180, local copies, waits for them, and re-layouts  26.1 us
    ppermute x8, starting transfers between devices, from_behind(): return lax.ppermute(shard, axis, pairs)  18.6 us
    add x4, local copies, waits for them, and re-layouts, on_device(): into_part + jnp.dot(key_gradient_lowrank, key_matrix[rows].T, preferred_e...  11.9 us
  transfers between devices with their start and end apart: 10, of which 1 were waited for; matrix products, arithmetic and copies ran while one was open for 13% of the time, Pallas kernels for 33%

profile of v2, /device:TPU:12, one launch (start us, length us, event | category | flops | bytes accessed | tf_op | source)
XLA Modules:
  0.0 560.4 jit_solution(7880592291553580539)
XLA Ops:
  8.0 2.2 copy.231
  17.9 2.3 copy.252
  20.2 4.2 fusion.61
  24.3 56.3 %shard_map.268 = (bf16[8,672,256]{2,1,0:T(8,128)(2,1)}, bf16[8,672,256]{2,1,0:T(8,128)(2,1)}) custom-call(bf16[672,256]{1,0:T(8,128)(2,1)} %get-tuple-element.107.a_ref, bf16[672,256]{1,0:T(8,128)(2,1)} %get-tuple-element.106.b_ref), custom_call_target="tpu_custom_call" | custom-call | bytes 96337920 | tf_op jit(solution)/shard_map/pallas_call | solution.py:108
  83.3 5.2 multiply_convert_fusion
  88.6 2.7 fusion.1
  92.3 2.3 fusion.3
  101.5 4.1 collective-permute-start
  109.5 2.3 collective-permute-start.3
  111.8 130.3 %shard_map.269 = (bf16[8,672,512]{2,1,0:T(8,128)(2,1)}, bf16[8,672,512]{2,1,0:T(8,128)(2,1)}) custom-call(bf16[672,512]{1,0:T(8,128)(2,1)} %get-tuple-element.25.a_ref, bf16[672,512]{1,0:T(8,128)(2,1)} %get-tuple-element.26.b_ref), custom_call_target="tpu_custom_call" | custom-call | bytes 192675840 | tf_op jit(solution)/shard_map/pallas_call | solution.py:108
  242.1 4.2 fusion.139
  248.7 4.8 fusion.123
  261.1 5.7 %fusion.13 = f32[2,2,256,1280]{2,3,1,0:T(8,128)} fusion(bf16[1280,2,128,1]{0,2,3,1:T(8,128)(2,1)} %bitcast.359, pred[256,1280]{0,1:T(8,128)(4,1)S(1)} %copy-done.51, bf16[256,2,2,64]{3,0,2,1:T(8,128)(2,1)} %bitcast.365, bf16[256,2,2,64]{3,0,2,1:T(8,128)(2,1)S(1)} %bitcast.363), kind=kOutput, calls=%fused_computation.34 | convolution fusion | flops 340003072 | bytes 6488064 | tf_op jit(solution)/shard_map/div | solution.py:401
  266.8 3.1 fusion.48
  276.1 27.4 %shard_map.270 = (f32[256,1344]{1,0:T(8,128)}, f32[256,128]{1,0:T(8,128)}) custom-call(bf16[4,256,1344]{2,1,0:T(8,128)(2,1)} %pad_maximum_fusion.1.parts_ref, f32[256,128]{1,0:T(8,128)} %pad.8.small_ref), custom_call_target="tpu_custom_call" | custom-call | tf_op jit(solution)/shard_map/pallas_call | solution.py:313
  303.6 3.2 fusion.33
  306.8 6.7 %all-reduce.2 = (f32[256,1]{0,1:T(1,128)S(1)}, f32[256,1]{0,1:T(1,128)S(1)}) all-reduce(f32[256,1]{0,1:T(1,128)S(1)} %bitcast.372, f32[256,1]{0,1:T(1,128)S(1)} %bitcast.371), channel_id=1, replica_groups=mesh['ctx'=8,'tp'=4] {'tp'}, use_global_device_ids=true, to_apply=%region_5.6 | all-reduce | flops 512 | bytes 4096 | tf_op jit(solution)/shard_map/psum | solution.py:534
  313.5 2.8 fusion.32
  318.8 5.1 fusion.124
  325.5 5.7 %fusion.122 = (bf16[2,672,512]{2,1,0:T(8,128)(2,1)}, bf16[2,672,512]{2,1,0:T(8,128)(2,1)}, bf16[2,672,512]{2,1,0:T(8,128)(2,1)}, bf16[2,672,512]{2,1,0:T(8,128)(2,1)}) fusion(bf16[8,672,512]{2,1,0:T(8,128)(2,1)} %get-tuple-element.27), kind=kLoop, calls=%fused_computation.238 | loop fusion | bytes 11010048 | tf_op jit(solution)/shard_map/slice | solution.py:594
  331.2 2.2 copy.280
  334.3 10.3 %all-gather.5.cloned.1.call-done = bf16[256,5376]{0,1:T(8,128)(2,1)} async-done(((bf16[256,1344]{0,1:T(8,128)(2,1)}), bf16[256,5376]{0,1:T(8,128)(2,1)}) %all-gather.5.cloned.1.call-update) | async-done | bytes 2752528 | tf_op jit(solution)/shard_map/all_gather | solution.py:542
  344.6 2.4 convolution_convert_fusion.4
  347.2 4.2 fusion.141
  352.5 3.6 fusion.40
  356.2 3.2 fusion.142
  359.4 9.9 %fusion.27 = f32[2,128,1280,1]{2,1,3,0:T(8,128)} fusion(f32[2,2,256,1280]{2,3,1,0:T(8,128)} %fusion.13, f32[2,1280,256,2]{2,1,3,0:T(8,128)} %fusion.142, bf16[256,2,2,64]{3,0,2,1:T(8,128)(2,1)} %bitcast.366, bf16[256,2,2,64]{3,0,2,1:T(8,128)(2,1)} %bitcast.364), kind=kOutput, calls=%fused_computation.56 | convolution fusion | flops 342624512 | bytes 12058624 | tf_op jit(solution)/shard_map/kgtl,tkgd->lkd/dot_general | solution.py:429
  369.3 9.4 %fusion.28 = f32[2,128,2,256]{3,1,2,0:T(8,128)} fusion(bf16[1280,2,128,1]{0,2,3,1:T(8,128)(2,1)} %bitcast.360, f32[2,2,256,1280]{2,3,1,0:T(8,128)} %fusion.13, f32[2,1280,256,2]{2,1,3,0:T(8,128)} %fusion.142), kind=kOutput, calls=%fused_computation.57 | convolution fusion | flops 342100224 | bytes 11665408 | tf_op jit(solution)/shard_map/kgtl,lkd->tkgd/dot_general | solution.py:426
  381.3 2.6 collective-permute-start.4
  383.9 2.5 collective-permute-start.5
  390.6 2.0 copy.312
  392.5 2.0 copy.313
  410.7 2.8 convolution_add_fusion.3
  413.5 2.9 copy.266
  416.5 2.8 convolution_add_fusion.2
  419.3 3.0 copy.268
  422.2 2.8 convolution_add_fusion.1
  425.0 3.0 copy.270
  428.0 2.8 convolution_add_fusion
  430.8 3.0 copy.272
  439.2 2.0 pad_maximum_fusion.2.parts_ref
  441.2 27.4 %shard_map.271 = (f32[256,1344]{1,0:T(8,128)}, f32[256,128]{1,0:T(8,128)}) custom-call(bf16[4,256,1344]{2,1,0:T(8,128)(2,1)} %pad_maximum_fusion.2.parts_ref, f32[256,128]{1,0:T(8,128)} %pad.9.small_ref), custom_call_target="tpu_custom_call" | custom-call | tf_op jit(solution)/shard_map/pallas_call | solution.py:313
  470.9 54.2 %shard_map.272 = (f32[4,8,8,1408]{3,2,1,0:T(8,128)}, f32[8,8,384]{2,1,0:T(8,128)}) custom-call(f32[64,1792]{1,0:T(8,128)} %concatenate.54.g_ref), custom_call_target="tpu_custom_call" | custom-call | tf_op jit(solution)/shard_map/pallas_call | solution.py:206
  528.7 2.3 fusion.82
  536.4 2.5 fusion.37
  538.9 7.5 %psum.23 = f32[256,1]{0,1:T(1,128)S(1)} all-reduce(f32[256,1]{0,1:T(1,128)S(1)} %bitcast.370), channel_id=1, replica_groups=mesh['ctx'=8,'tp'=4] {'tp'}, use_global_device_ids=true, to_apply=%region_12.13 | all-reduce | flops 256 | bytes 2048 | tf_op jit(solution)/shard_map/psum | solution.py:624
  546.9 3.0 fusion.34
  549.9 2.9 copy.281
  (310 shorter events, 85.3 us)
Async XLA Ops:
  7.2 296.4 %copy-start = (bf16[16,5376]{1,0:T(8,128)(2,1)S(1)}, bf16[16,5376]{1,0:T(8,128)(2,1)}, u32[]{:S(2)}) copy-start(bf16[16,5376]{1,0:T(8,128)(2,1)} %param.41) | copy-start | bytes 516100
  7.2 3.1 copy-start.78
  7.2 3.1 copy-start.81
  7.2 81.3 %all-gather.3.cloned.1.call-start = ((), (), s32[]{:S(2)}) async-start(), calls=%async_computation | async-start | bytes 3440640 | tf_op jit(solution)/shard_map/all_gather | solution.py:473
  7.9 336.7 %all-gather.5.cloned.1.call-start = ((), (), s32[]{:S(2)}) async-start(), calls=%async_computation.1 | async-start | bytes 3440640 | tf_op jit(solution)/shard_map/all_gather | solution.py:542
  12.1 2.5 copy-start.79
  14.6 85.9 %copy-start.45 = (f32[256,64]{0,1:T(8,128)}, f32[256,64]{0,1:T(8,128)S(1)}, u32[]{:S(2)}) copy-start(f32[256,64]{0,1:T(8,128)S(1)} %copy.237) | copy-start | bytes 196612
  20.2 63.2 %copy-start.11 = (f32[672,512]{1,0:T(8,128)S(1)}, f32[672,512]{1,0:T(8,128)}, u32[]{:S(2)}) copy-start(f32[672,512]{1,0:T(8,128)} %copy.233) | copy-start | bytes 4128772
  83.3 9.0 %copy-start.62 = (f32[5376]{0:T(1024)S(1)}, f32[5376]{0:T(1024)}, u32[]{:S(2)}) copy-start(f32[5376]{0:T(1024)} %param.23) | copy-start | bytes 64516
  88.6 3.8 copy-start.5
  101.5 153.7 %collective-permute-start = (bf16[2,256,256]{1,2,0:T(8,128)(2,1)}, bf16[2,256,256]{1,2,0:T(8,128)(2,1)}, u32[]{:S(2)}, u32[]{:S(2)}) collective-permute-start(bf16[2,256,256]{1,2,0:T(8,128)(2,1)} %pad_maximum_fusion.4), channel_id=1, source_target_pairs={{0,16},{4,20},{8,24},{12,28},{1,17},{5,21},{9,25},{13,29},{2,18},{... | collective-permute-start | bytes 786440 | tf_op jit(solution)/shard_map/ppermute | solution.py:44
  105.6 150.6 %collective-permute-start.1 = (bf16[2,256,256]{1,2,0:T(8,128)(2,1)}, bf16[2,256,256]{1,2,0:T(8,128)(2,1)}, u32[]{:S(2)}, u32[]{:S(2)}) collective-permute-start(bf16[2,256,256]{1,2,0:T(8,128)(2,1)} %pad_maximum_fusion.4), channel_id=1, source_target_pairs={{0,12},{4,16},{8,20},{12,24},{16,28},{1,13},{5,17},{9,21},{13,25},... | collective-permute-start | bytes 786440 | tf_op jit(solution)/shard_map/ppermute | solution.py:44
  107.5 149.7 %collective-permute-start.2 = (bf16[2,256,256]{1,2,0:T(8,128)(2,1)}, bf16[2,256,256]{1,2,0:T(8,128)(2,1)}, u32[]{:S(2)}, u32[]{:S(2)}) collective-permute-start(bf16[2,256,256]{1,2,0:T(8,128)(2,1)} %pad_maximum_fusion.4), channel_id=1, source_target_pairs={{0,8},{4,12},{8,16},{12,20},{16,24},{20,28},{1,9},{5,13},{9,17},{1... | collective-permute-start | bytes 786440 | tf_op jit(solution)/shard_map/ppermute | solution.py:44
  109.5 148.7 %collective-permute-start.3 = (bf16[2,256,256]{1,2,0:T(8,128)(2,1)}, bf16[2,256,256]{1,2,0:T(8,128)(2,1)}, u32[]{:S(2)}, u32[]{:S(2)}) collective-permute-start(bf16[2,256,256]{1,2,0:T(8,128)(2,1)} %pad_maximum_fusion.4), channel_id=1, source_target_pairs={{0,4},{4,8},{8,12},{12,16},{16,20},{20,24},{24,28},{1,5},{5,9},{9,... | collective-permute-start | bytes 786440 | tf_op jit(solution)/shard_map/ppermute | solution.py:44
  242.1 4.2 copy-start.52
  247.3 6.2 %copy-start.20 = (f32[256,512]{1,0:T(8,128)}, f32[256,512]{1,0:T(8,128)S(1)}, u32[]{:S(2)}) copy-start(f32[256,512]{1,0:T(8,128)S(1)} %fusion.46) | copy-start | bytes 1572868
  248.7 4.8 copy-start.43
  248.7 4.8 copy-start.69
  248.7 5.1 copy-start.36
  248.7 5.1 copy-start.39
  254.4 6.6 %copy-start.53 = (bf16[256,4,64]{2,0,1:T(8,128)(2,1)}, bf16[256,4,64]{2,0,1:T(8,128)(2,1)S(1)}, u32[]{:S(2)}) copy-start(bf16[256,4,64]{2,0,1:T(8,128)(2,1)S(1)} %copy.242) | copy-start | bytes 393220
  261.1 5.7 %copy-start.6 = (bf16[1,1280,256]{1,2,0:T(8,128)(2,1)}, bf16[1,1280,256]{1,2,0:T(8,128)(2,1)S(1)}, u32[]{:S(2)}) copy-start(bf16[1,1280,256]{1,2,0:T(8,128)(2,1)S(1)} %get-tuple-element.115) | copy-start | bytes 1966084
  266.8 3.2 copy-start.18
  276.1 27.5 %copy-start.4 = (bf16[256,1344]{1,0:T(8,128)(2,1)S(1)}, bf16[256,1344]{1,0:T(8,128)(2,1)}, u32[]{:S(2)}) copy-start(bf16[256,1344]{1,0:T(8,128)(2,1)} %copy.252) | copy-start | bytes 2064388
  303.6 9.9 %copy-start.3 = (bf16[256,1344]{1,0:T(8,128)(2,1)S(1)}, bf16[256,1344]{1,0:T(8,128)(2,1)}, u32[]{:S(2)}) copy-start(bf16[256,1344]{1,0:T(8,128)(2,1)} %copy.231) | copy-start | bytes 2064388
  316.3 2.5 copy-start.70
  318.8 5.1 copy-start.42
  318.8 5.9 %copy-start.65 = (f32[256,4]{0,1:T(4,128)S(1)}, f32[256,4]{0,1:T(4,128)}, u32[]{:S(2)}) copy-start(f32[256,4]{0,1:T(4,128)} %get-tuple-element.132) | copy-start | bytes 12292
  344.6 2.6 copy-start.2
  347.2 4.2 copy-start.60
  352.5 3.6 copy-start.7
  352.5 3.6 copy-start.34
  380.3 9.5 %copy-start.49 = (f32[2,128,2,256]{3,1,2,0:T(8,128)S(1)}, f32[2,128,2,256]{3,1,2,0:T(8,128)}, u32[]{:S(2)}) copy-start(f32[2,128,2,256]{3,1,2,0:T(8,128)} %fusion.28) | copy-start | bytes 1572868
  381.3 13.2 %copy-start.37 = (f32[256,64]{1,0:T(8,128)S(1)}, f32[256,64]{1,0:T(8,128)}, u32[]{:S(2)}) copy-start(f32[256,64]{1,0:T(8,128)} %copy-done.35) | copy-start | bytes 196612
  381.3 25.4 %collective-permute-start.4 = (bf16[2,256,256]{1,2,0:T(8,128)(2,1)}, bf16[2,256,256]{1,2,0:T(8,128)(2,1)}, u32[]{:S(2)}, u32[]{:S(2)}) collective-permute-start(bf16[2,256,256]{1,2,0:T(8,128)(2,1)} %get-tuple-element.108), channel_id=1, source_target_pairs={{4,0},{8,4},{12,8},{16,12},{20,16},{24,20},{28,24},{5,1},{9,5},{13... | collective-permute-start | bytes 786440 | tf_op jit(solution)/shard_map/ppermute | solution.py:44
  383.9 22.9 %collective-permute-start.5 = (bf16[2,256,256]{1,2,0:T(8,128)(2,1)}, bf16[2,256,256]{1,2,0:T(8,128)(2,1)}, u32[]{:S(2)}, u32[]{:S(2)}) collective-permute-start(bf16[2,256,256]{1,2,0:T(8,128)(2,1)} %get-tuple-element.111), channel_id=1, source_target_pairs={{8,0},{12,4},{16,8},{20,12},{24,16},{28,20},{9,1},{13,5},{17,9},{2... | collective-permute-start | bytes 786440 | tf_op jit(solution)/shard_map/ppermute | solution.py:44
  386.3 20.4 %collective-permute-start.6 = (bf16[2,256,256]{1,2,0:T(8,128)(2,1)}, bf16[2,256,256]{1,2,0:T(8,128)(2,1)}, u32[]{:S(2)}, u32[]{:S(2)}) collective-permute-start(bf16[2,256,256]{1,2,0:T(8,128)(2,1)} %get-tuple-element.110), channel_id=1, source_target_pairs={{12,0},{16,4},{20,8},{24,12},{28,16},{13,1},{17,5},{21,9},{25,13},... | collective-permute-start | bytes 786440 | tf_op jit(solution)/shard_map/ppermute | solution.py:44
  388.3 18.5 %collective-permute-start.7 = (bf16[2,256,256]{1,2,0:T(8,128)(2,1)}, bf16[2,256,256]{1,2,0:T(8,128)(2,1)}, u32[]{:S(2)}, u32[]{:S(2)}) collective-permute-start(bf16[2,256,256]{1,2,0:T(8,128)(2,1)} %get-tuple-element.109), channel_id=1, source_target_pairs={{16,0},{20,4},{24,8},{28,12},{17,1},{21,5},{25,9},{29,13},{18,2},{... | collective-permute-start | bytes 786440 | tf_op jit(solution)/shard_map/ppermute | solution.py:44
  392.5 3.5 copy-start.71
  404.2 2.6 copy-start.19
  413.5 2.9 copy-start.28
  419.3 3.0 copy-start.27
  425.0 3.0 copy-start.26
  430.8 3.0 copy-start.33
  441.2 28.4 %copy-start.67 = (f32[256]{0:T(256)S(1)}, f32[256]{0:T(256)}, u32[]{:S(2)}) copy-start(f32[256]{0:T(256)} %copy-done.66) | copy-start | bytes 3076
  536.3 10.0 %copy-start.73 = (f32[256]{0:T(256)S(1)}, f32[256]{0:T(256)}, u32[]{:S(2)}) copy-start(f32[256]{0:T(256)} %get-tuple-element.140) | copy-start | bytes 3076
  536.3 10.6 %copy-start.72 = (f32[256]{0:T(256)S(1)}, f32[256]{0:T(256)}, u32[]{:S(2)}) copy-start(f32[256]{0:T(256)} %get-tuple-element.141) | copy-start | bytes 3076
  546.9 6.4 %copy-start.1 = (bf16[16,5376]{1,0:T(8,128)(2,1)S(1)}, bf16[16,5376]{1,0:T(8,128)(2,1)}, u32[]{:S(2)}) copy-start(bf16[16,5376]{1,0:T(8,128)(2,1)} %param.41) | copy-start | bytes 516100
  (46 other events, 64.1 us)
Sparse Core Ops, SparseCore 0:
  9.6 27.3 all-gather.2
  317.6 26.9 all-gather.4

commit v3 on v2

--- a/solution.py
+++ b/solution.py
@@ -470,6 +470,10 @@
     v_part = dequantize(kv_codes[1], kv_scodes[1], kv_second[1], row_start)
     o_part = dequantize(o_codes, o_scodes, o_second, row_start)
     key_matrix, value_matrix = gather_pair(k_part, v_part, 1)
+    q_part, o_part, key_matrix, value_matrix = lax.optimization_barrier(
+        (q_part, o_part, key_matrix, value_matrix)
+    )
+    query_matrix, output_matrix = gather_pair(q_part, o_part, 2)
     whole_tokens = lax.all_gather(tokens, "tp", axis=1, tiled=True)
     wide = whole_tokens.astype(jnp.float32)
     row_scale = lax.rsqrt(jnp.mean(wide * wide, axis=1, keepdims=True) + EPSILON)
@@ -483,6 +487,9 @@
     value_lowrank = jnp.dot(
         normalized_input, kv_down[1], preferred_element_type=jnp.float32
     ).astype(jnp.bfloat16)
+    query_rows = jnp.dot(
+        normalized_input, query_matrix, preferred_element_type=jnp.float32
+    ) + ADAPTER_SCALE * jnp.dot(query_lowrank, query_up, preferred_element_type=jnp.float32)
     key = jnp.dot(
         normalized_input, key_matrix, preferred_element_type=jnp.float32
     ) + ADAPTER_SCALE * jnp.dot(key_lowrank, key_value_up[0], preferred_element_type=jnp.float32)
@@ -493,23 +500,18 @@
     query_pos = ctx_rank * count + jnp.arange(count, dtype=jnp.int32)
     key_pos = ctx_rank * count - WINDOW_TOKENS + jnp.arange(WINDOW_TOKENS + count, dtype=jnp.int32)
     cosine, sine = rope_tables(query_pos)
+    q_heads = query_rows.reshape(count, q_heads_here, HEAD_SIZE)
+    q_normed, q_scale = head_norm(q_heads, query_gain)
+    q_rot = rotate(q_normed, cosine, sine).astype(jnp.bfloat16)
     key_head_rows = key.reshape(count, kv_heads_here, HEAD_SIZE)
     k_normed, k_scale = head_norm(key_head_rows, key_gain)
     k_rot = rotate(k_normed, cosine, sine).astype(jnp.bfloat16)
     piece_rows = min(WINDOW_TOKENS, count)
     pieces = WINDOW_TOKENS // piece_rows
     stacked = jnp.stack([k_rot.reshape(count, kv_width), value_rows])
-    q_part, o_part, stacked = lax.optimization_barrier((q_part, o_part, stacked))
     arrived = []
     for offset in range(pieces, 0, -1):
         arrived.append(from_behind(stacked, "ctx", offset))
-    query_matrix, output_matrix = gather_pair(q_part, o_part, 2)
-    query_rows = jnp.dot(
-        normalized_input, query_matrix, preferred_element_type=jnp.float32
-    ) + ADAPTER_SCALE * jnp.dot(query_lowrank, query_up, preferred_element_type=jnp.float32)
-    q_heads = query_rows.reshape(count, q_heads_here, HEAD_SIZE)
-    q_normed, q_scale = head_norm(q_heads, query_gain)
-    q_rot = rotate(q_normed, cosine, sine).astype(jnp.bfloat16)
     window = jnp.concatenate(arrived + [stacked], axis=1)
     window_keys = window[0].reshape(WINDOW_TOKENS + count, kv_heads_here, HEAD_SIZE)
     window_values = window[1].reshape(WINDOW_TOKENS + count, kv_heads_here, HEAD_SIZE)
@@ -587,28 +589,22 @@
     value_mixture = jnp.dot(
         value_gradient_lowrank, key_value_up[1].T, preferred_element_type=jnp.float32
     )
-    into_parts = []
-    for k in range(sharers):
-        rows = slice(k * share, (k + 1) * share)
-        into_part = jnp.dot(
-            query_gradient_lowrank, query_matrix[rows].T, preferred_element_type=jnp.float32
-        )
-        into_part = into_part + jnp.dot(
-            key_gradient_lowrank, key_matrix[rows].T, preferred_element_type=jnp.float32
-        )
-        into_part = into_part + jnp.dot(
-            value_gradient_lowrank, value_matrix[rows].T, preferred_element_type=jnp.float32
-        )
-        into_parts.append(into_part.astype(jnp.bfloat16))
-    into_mine, mixture_sum = share_sums(
-        jnp.stack(into_parts),
-        jnp.concatenate([query_mixture, key_mixture, value_mixture], axis=1),
-        5,
-    )
-    query_mixture, key_mixture, value_mixture = jnp.split(mixture_sum, 3, axis=1)
+    into_part = jnp.dot(query_gradient_lowrank, query_matrix.T, preferred_element_type=jnp.float32)
+    into_part = into_part + jnp.dot(
+        key_gradient_lowrank, key_matrix.T, preferred_element_type=jnp.float32
+    )
+    into_part = into_part + jnp.dot(
+        value_gradient_lowrank, value_matrix.T, preferred_element_type=jnp.float32
+    )
+    query_mixture, key_mixture, value_mixture = lax.psum(
+        (query_mixture, key_mixture, value_mixture), "tp"
+    )
     query_mixture = query_mixture.astype(jnp.bfloat16)
     key_mixture = key_mixture.astype(jnp.bfloat16)
     value_mixture = value_mixture.astype(jnp.bfloat16)
+    into_mine = lax.psum_scatter(
+        into_part.astype(jnp.bfloat16), "tp", scatter_dimension=1, tiled=True
+    ).astype(jnp.float32)
     q_down_mine = lax.dynamic_slice_in_dim(q_down, column_start, share, 0)
     k_down_mine = lax.dynamic_slice_in_dim(kv_down[0], column_start, share, 0)
     v_down_mine = lax.dynamic_slice_in_dim(kv_down[1], column_start, share, 0)

time: 567 us -> 507 us (0.89)
  Pallas kernels: 296 us -> 244 us
  waiting for transfers between devices: 11 us -> 47.4 us
  local copies, waits for them, and re-layouts: 78.5 us -> 50.3 us
  matrix products: 88.5 us -> 66.6 us
  blocking collectives: 14.2 us -> 24.6 us
    pallas_call x2 -> x1, Pallas kernels: 54.8 us -> 27.3 us  [share_sums(): pl.pallas_call(functools.partial(share_kernel, chunks), out_shape=[jax.Sh...]
    pallas_call x2, Pallas kernels: 187 us -> 162 us  [gather_pair(): pl.pallas_call(functools.partial(gather_kernel, devices, chunks), out_sha...]
    ppermute x8, waiting for transfers between devices: 0.03 us -> 22.1 us  [from_behind(): return lax.ppermute(shard, axis, pairs)]
    dot_general x12 -> x3, matrix products: 20.9 us -> 4.89 us  [the longest x1 2.39 us: on_device(): jnp.dot(value_gradient_lowrank, value_matrix.T, preferred_element_type=jn...]
    all_gather x1, waiting for transfers between devices: 10.3 us -> 24.6 us  [on_device(): output_gradient = lax.all_gather(grad_mine, 'tp', axis=1, tiled=True)]
    add x4 -> x0, local copies, waits for them, and re-layouts: 11.9 us -> none  [on_device(): into_part + jnp.dot(key_gradient_lowrank, key_matrix[rows].T, preferred_e...]
    psum x0 -> x1, blocking collectives: none -> 10.8 us  [on_device(): lax.psum((query_mixture, key_mixture, value_mixture), 'tp')]
    slice x2 -> x0, local copies, waits for them, and re-layouts: 10.8 us -> none  [the longest x1 5.7 us: on_device(): query_matrix[rows]]
  transfers between devices with their start and end apart: 10 -> 11, of which waited for: 1 -> 7; matrix products, arithmetic and copies ran while one was open for 13% -> 13% of each run, Pallas kernels for 33% -> 43%
where the time goes in v3:
time: 507 us; the launch traced here: 502 us
  Pallas kernels  244 us (48%)
  matrix products  66.6 us (13%)
  local copies, waits for them, and re-layouts  50.3 us (10%)
  waiting for transfers between devices  47.4 us (9%)
  other arithmetic  34.8 us (7%)
  blocking collectives  24.6 us (5%)
  starting transfers between devices  19 us (4%)
  between operations  15.3 us (3%)
    pallas_call x2, Pallas kernels, gather_pair(): pl.pallas_call(functools.partial(gather_kernel, devices, chunks), out_sha...  162 us
    pallas_call x1, Pallas kernels, reduce_gradients(): pl.pallas_call(functools.partial(reduce_kernel, devices, sharers, split),...  54.4 us
    pallas_call x1, Pallas kernels, share_sums(): pl.pallas_call(functools.partial(share_kernel, chunks), out_shape=[jax.Sh...  27.3 us
    all_gather x1, waiting for transfers between devices, on_device(): output_gradient = lax.all_gather(grad_mine, 'tp', axis=1, tiled=True)  24.6 us
    ppermute x8, waiting for transfers between devices, from_behind(): return lax.ppermute(shard, axis, pairs)  22.1 us
    unnamed x159, local copies, waits for them, and re-layouts  21.8 us
    ppermute x8, starting transfers between devices, from_behind(): return lax.ppermute(shard, axis, pairs)  18.4 us
    psum x1, blocking collectives, on_device(): lax.psum((query_mixture, key_mixture, value_mixture), 'tp')  10.8 us
  transfers between devices with their start and end apart: 11, of which 7 were waited for; matrix products, arithmetic and copies ran while one was open for 13% of the time, Pallas kernels for 43%

profile of v3, /device:TPU:12, one launch (start us, length us, event | category | flops | bytes accessed | tf_op | source)
XLA Modules:
  0.0 502.1 jit_solution(6604795492896852555)
XLA Ops:
  15.9 4.1 fusion.55
  20.0 56.3 %shard_map.268 = (bf16[8,672,256]{2,1,0:T(8,128)(2,1)}, bf16[8,672,256]{2,1,0:T(8,128)(2,1)}) custom-call(bf16[672,256]{1,0:T(8,128)(2,1)} %get-tuple-element.96.a_ref, bf16[672,256]{1,0:T(8,128)(2,1)} %get-tuple-element.95.b_ref), custom_call_target="tpu_custom_call" | custom-call | bytes 96337920 | tf_op jit(solution)/shard_map/pallas_call | solution.py:108
  76.3 5.6 %multiply_convert_fusion = (bf16[672,512]{1,0:T(8,128)(2,1)}, bf16[672,512]{1,0:T(8,128)(2,1)}) fusion(f32[672,512]{1,0:T(8,128)} %copy.189, s32[672,512]{1,0:T(8,128)} %param.33, f32[672,512]{1,0:T(8,128)S(1)} %copy-done.15, s32[672,512]{1,0:T(8,128)} %param.27), kind=kLoop, calls=%fused_computation.61 | loop fusion | flops 23396352 | bytes 6881280 | tf_op jit(solution)/shard_map/convert_element_type | solution.py:346
  83.1 106.0 %shard_map.269 = (bf16[8,672,512]{2,1,0:T(8,128)(2,1)}, bf16[8,672,512]{2,1,0:T(8,128)(2,1)}) custom-call(bf16[672,512]{1,0:T(8,128)(2,1)} %get-tuple-element.25.a_ref, bf16[672,512]{1,0:T(8,128)(2,1)} %get-tuple-element.26.b_ref), custom_call_target="tpu_custom_call" | custom-call | bytes 192675840 | tf_op jit(solution)/shard_map/pallas_call | solution.py:108
  189.9 5.2 %fusion.122 = (bf16[2,672,512]{2,1,0:T(8,128)(2,1)}, bf16[2,672,512]{2,1,0:T(8,128)(2,1)}, bf16[2,672,512]{2,1,0:T(8,128)(2,1)}, bf16[2,672,512]{2,1,0:T(8,128)(2,1)}) fusion(bf16[8,672,512]{2,1,0:T(8,128)(2,1)} %get-tuple-element.28), kind=kLoop, calls=%fused_computation.227 | loop fusion | bytes 11010048 | tf_op jit(solution)/shard_map/slice | solution.py:525
  195.0 1.6 fusion.39
  196.6 2.7 fusion.3
  200.5 2.3 fusion.5
  209.5 4.1 collective-permute-start
  213.5 1.9 collective-permute-start.1
  215.5 1.9 collective-permute-start.2
  217.4 2.3 collective-permute-start.3
  219.7 1.6 fusion.129
  225.5 2.7 collective-permute-done
  229.2 4.6 collective-permute-done.1
  234.8 4.6 collective-permute-done.2
  240.5 4.6 collective-permute-done.3
  246.1 5.9 %fusion.15 = f32[2,2,256,1280]{2,3,1,0:T(8,128)} fusion(bf16[1280,2,128,1]{0,2,3,1:T(8,128)(2,1)S(1)} %bitcast.325, pred[256,1280]{0,1:T(8,128)(4,1)} %fusion.39, bf16[256,2,2,64]{3,0,2,1:T(8,128)(2,1)} %bitcast.330, bf16[256,2,2,64]{3,0,2,1:T(8,128)(2,1)} %bitcast.328), kind=kOutput, calls=%fused_computation.29 | convolution fusion | flops 340003072 | bytes 6488064 | tf_op jit(solution)/shard_map/div | solution.py:401
  252.0 3.1 fusion.42
  260.1 1.8 pad_maximum_fusion.1.parts_ref
  261.9 27.3 %shard_map.270 = (f32[256,1344]{1,0:T(8,128)}, f32[256,128]{1,0:T(8,128)}) custom-call(bf16[4,256,1344]{2,1,0:T(8,128)(2,1)} %pad_maximum_fusion.1.parts_ref, f32[256,128]{1,0:T(8,128)} %pad.4.small_ref), custom_call_target="tpu_custom_call" | custom-call | tf_op jit(solution)/shard_map/pallas_call | solution.py:313
  289.2 3.2 fusion.27
  292.4 6.3 %all-reduce.2 = (f32[256,1]{0,1:T(1,128)S(1)}, f32[256,1]{0,1:T(1,128)S(1)}) all-reduce(f32[256,1]{0,1:T(1,128)S(1)} %bitcast.337, f32[256,1]{0,1:T(1,128)S(1)} %bitcast.336), channel_id=1, replica_groups=mesh['ctx'=8,'tp'=4] {'tp'}, use_global_device_ids=true, to_apply=%region_5.6 | all-reduce | flops 512 | bytes 4096 | tf_op jit(solution)/shard_map/psum | solution.py:536
  298.7 2.8 fusion.26
  305.1 24.6 %all-gather.5.cloned.1.call-done = bf16[256,5376]{0,1:T(8,128)(2,1)} async-done(((bf16[256,1344]{0,1:T(8,128)(2,1)}), bf16[256,5376]{0,1:T(8,128)(2,1)}) %all-gather.5.cloned.1.call-update) | async-done | bytes 2752528 | tf_op jit(solution)/shard_map/all_gather | solution.py:544
  329.7 2.4 convolution_convert_fusion.4
  332.3 4.2 fusion.131
  336.9 3.6 fusion.34
  340.5 3.2 fusion.132
  343.8 9.8 %fusion.21 = f32[2,128,1280,1]{2,1,3,0:T(8,128)} fusion(f32[2,2,256,1280]{2,3,1,0:T(8,128)} %fusion.15, f32[2,1280,256,2]{2,1,3,0:T(8,128)} %fusion.132, bf16[256,2,2,64]{3,0,2,1:T(8,128)(2,1)S(1)} %bitcast.331, bf16[256,2,2,64]{3,0,2,1:T(8,128)(2,1)S(1)} %bitcast.329), kind=kOutput, calls=%fused_computation.43 | convolution fusion | flops 342624512 | bytes 12058624 | tf_op jit(solution)/shard_map/kgtl,tkgd->lkd/dot_general | solution.py:429
  353.6 9.3 %fusion.22 = f32[2,128,2,256]{3,1,2,0:T(8,128)} fusion(bf16[1280,2,128,1]{0,2,3,1:T(8,128)(2,1)S(1)} %bitcast.326, f32[2,2,256,1280]{2,3,1,0:T(8,128)} %fusion.15, f32[2,1280,256,2]{2,1,3,0:T(8,128)} %fusion.132), kind=kOutput, calls=%fused_computation.44 | convolution fusion | flops 342100224 | bytes 11665408 | tf_op jit(solution)/shard_map/kgtl,lkd->tkgd/dot_general | solution.py:426
  362.9 1.7 fusion.13
  365.5 2.4 collective-permute-start.4
  368.0 2.5 collective-permute-start.5
  370.5 1.9 collective-permute-start.6
  374.7 1.9 copy.258
  376.7 2.0 copy.259
  378.6 1.7 multiply_add_fusion
  380.3 1.7 multiply_reduce_fusion.1
  383.5 1.6 fusion.133
  385.2 4.9 collective-permute-done.6
  394.8 2.4 fusion.2
  401.4 10.8 %all-reduce.1 = (bf16[256,16]{0,1:T(8,128)(2,1)S(1)}, bf16[256,16]{0,1:T(8,128)(2,1)S(1)}, bf16[256,16]{0,1:T(8,128)(2,1)S(1)}) all-reduce(f32[256,16]{0,1:T(8,128)S(1)} %fusion.134, f32[256,16]{0,1:T(8,128)S(1)} %fusion.89, f32[256,16]{0,1:T(8,128)S(1)} %fusion.86), channel_id=1, replica_groups=mesh['ctx'=8,'tp'=4] {'tp'}, use_global_device_ids=true, to_apply=%region_12.13 | all-reduce | flops 12288 | bytes 73728 | tf_op jit(solution)/shard_map/psum | solution.py:599
  413.6 54.4 %shard_map.271 = (f32[4,8,8,1408]{3,2,1,0:T(8,128)}, f32[8,8,384]{2,1,0:T(8,128)}) custom-call(f32[64,1792]{1,0:T(8,128)} %concatenate.50.g_ref), custom_call_target="tpu_custom_call" | custom-call | tf_op jit(solution)/shard_map/pallas_call | solution.py:206
  478.2 2.2 copy.257
  480.5 2.3 fusion.31
  482.8 7.5 %psum.47 = f32[256,1]{0,1:T(1,128)S(1)} all-reduce(f32[256,1]{0,1:T(1,128)S(1)} %bitcast.335), channel_id=1, replica_groups=mesh['ctx'=8,'tp'=4] {'tp'}, use_global_device_ids=true, to_apply=%region_16.17 | all-reduce | flops 256 | bytes 2048 | tf_op jit(solution)/shard_map/psum | solution.py:620
  492.5 2.9 copy.229
  (274 shorter events, 62.4 us)
Async XLA Ops:
  7.2 282.1 %copy-start = (bf16[16,5376]{1,0:T(8,128)(2,1)S(1)}, bf16[16,5376]{1,0:T(8,128)(2,1)}, u32[]{:S(2)}) copy-start(bf16[16,5376]{1,0:T(8,128)(2,1)} %param.41) | copy-start | bytes 516100
  7.2 189.4 %all-gather.3.cloned.1.call-start = ((), (), s32[]{:S(2)}) async-start(), calls=%async_computation.1 | async-start | bytes 3440640 | tf_op jit(solution)/shard_map/all_gather | solution.py:477
  7.9 321.8 %all-gather.5.cloned.1.call-start = ((), (), s32[]{:S(2)}) async-start(), calls=%async_computation.2 | async-start | bytes 3440640 | tf_op jit(solution)/shard_map/all_gather | solution.py:544
  9.5 289.2 %copy-start.3 = (bf16[256,1344]{1,0:T(8,128)(2,1)}, bf16[256,1344]{1,0:T(8,128)(2,1)S(1)}, u32[]{:S(2)}) copy-start(bf16[256,1344]{1,0:T(8,128)(2,1)S(1)} %copy.187) | copy-start | bytes 2064388
  15.8 60.4 %copy-start.15 = (f32[672,512]{1,0:T(8,128)S(1)}, f32[672,512]{1,0:T(8,128)}, u32[]{:S(2)}) copy-start(f32[672,512]{1,0:T(8,128)} %copy.188) | copy-start | bytes 4128772
  76.3 6.4 %copy-start.32 = (bf16[256,1344]{0,1:T(8,128)(2,1)S(1)}, bf16[256,1344]{0,1:T(8,128)(2,1)}, u32[]{:S(2)}) copy-start(bf16[256,1344]{0,1:T(8,128)(2,1)} %param.22) | copy-start | bytes 2064388
  82.7 125.8 %copy-start.35 = (f32[256,64]{0,1:T(8,128)}, f32[256,64]{0,1:T(8,128)S(1)}, u32[]{:S(2)}) copy-start(f32[256,64]{0,1:T(8,128)S(1)} %copy.193) | copy-start | bytes 196612
  83.1 215.7 %copy-start.5 = (bf16[256,1344]{1,0:T(8,128)(2,1)}, bf16[256,1344]{1,0:T(8,128)(2,1)S(1)}, u32[]{:S(2)}) copy-start(bf16[256,1344]{1,0:T(8,128)(2,1)S(1)} %copy.208) | copy-start | bytes 2064388
  195.0 5.4 %copy-start.49 = (f32[5376]{0:T(1024)S(1)}, f32[5376]{0:T(1024)}, u32[]{:S(2)}) copy-start(f32[5376]{0:T(1024)} %param.23) | copy-start | bytes 64516
  196.6 3.9 copy-start.7
  203.2 3.0 copy-start.46
  203.2 3.9 copy-start.26
  205.0 14.7 %slice-start = ((s8[5505024]{0:T(1024)(128)(4,1)}), s8[4194304]{0:T(1024)(128)(4,1)S(1)}, s32[]{:S(2)}) async-start(s8[5505024]{0:T(1024)(128)(4,1)} %bitcast.279), calls=%async_computation.4 | async-start | bytes 8388608
  207.1 12.6 %slice-start.1 = ((s8[5505024]{0:T(1024)(128)(4,1)}), s8[1310720]{0:T(1024)(128)(4,1)S(1)}, s32[]{:S(2)}) async-start(s8[5505024]{0:T(1024)(128)(4,1)} %bitcast.279), calls=%async_computation.5 | async-start | bytes 2621440
  209.5 18.8 %collective-permute-start = (bf16[2,256,256]{1,2,0:T(8,128)(2,1)}, bf16[2,256,256]{1,2,0:T(8,128)(2,1)}, u32[]{:S(2)}, u32[]{:S(2)}) collective-permute-start(bf16[2,256,256]{1,2,0:T(8,128)(2,1)} %pad_maximum_fusion.3), channel_id=1, source_target_pairs={{0,16},{4,20},{8,24},{12,28},{1,17},{5,21},{9,25},{13,29},{2,18},{... | collective-permute-start | bytes 786440 | tf_op jit(solution)/shard_map/ppermute | solution.py:44
  213.5 20.3 %collective-permute-start.1 = (bf16[2,256,256]{1,2,0:T(8,128)(2,1)}, bf16[2,256,256]{1,2,0:T(8,128)(2,1)}, u32[]{:S(2)}, u32[]{:S(2)}) collective-permute-start(bf16[2,256,256]{1,2,0:T(8,128)(2,1)} %pad_maximum_fusion.3), channel_id=1, source_target_pairs={{0,12},{4,16},{8,20},{12,24},{16,28},{1,13},{5,17},{9,21},{13,25},... | collective-permute-start | bytes 786440 | tf_op jit(solution)/shard_map/ppermute | solution.py:44
  215.5 24.0 %collective-permute-start.2 = (bf16[2,256,256]{1,2,0:T(8,128)(2,1)}, bf16[2,256,256]{1,2,0:T(8,128)(2,1)}, u32[]{:S(2)}, u32[]{:S(2)}) collective-permute-start(bf16[2,256,256]{1,2,0:T(8,128)(2,1)} %pad_maximum_fusion.3), channel_id=1, source_target_pairs={{0,8},{4,12},{8,16},{12,20},{16,24},{20,28},{1,9},{5,13},{9,17},{1... | collective-permute-start | bytes 786440 | tf_op jit(solution)/shard_map/ppermute | solution.py:44
  217.4 27.6 %collective-permute-start.3 = (bf16[2,256,256]{1,2,0:T(8,128)(2,1)}, bf16[2,256,256]{1,2,0:T(8,128)(2,1)}, u32[]{:S(2)}, u32[]{:S(2)}) collective-permute-start(bf16[2,256,256]{1,2,0:T(8,128)(2,1)} %pad_maximum_fusion.3), channel_id=1, source_target_pairs={{0,4},{4,8},{8,12},{12,16},{16,20},{20,24},{24,28},{1,5},{5,9},{9,... | collective-permute-start | bytes 786440 | tf_op jit(solution)/shard_map/ppermute | solution.py:44
  246.1 5.9 %copy-start.33 = (bf16[1,1280,256]{1,2,0:T(8,128)(2,1)}, bf16[1,1280,256]{1,2,0:T(8,128)(2,1)S(1)}, u32[]{:S(2)}) copy-start(bf16[1,1280,256]{1,2,0:T(8,128)(2,1)S(1)} %get-tuple-element.103) | copy-start | bytes 1966084
  246.1 5.9 %copy-start.13 = (bf16[1,1280,256]{1,2,0:T(8,128)(2,1)}, bf16[1,1280,256]{1,2,0:T(8,128)(2,1)S(1)}, u32[]{:S(2)}) copy-start(bf16[1,1280,256]{1,2,0:T(8,128)(2,1)S(1)} %get-tuple-element.104) | copy-start | bytes 1966084
  252.0 3.2 copy-start.19
  301.6 30.6 %copy-start.11 = (bf16[256,1344]{1,0:T(8,128)(2,1)}, bf16[256,1344]{1,0:T(8,128)(2,1)S(1)}, u32[]{:S(2)}) copy-start(bf16[256,1344]{1,0:T(8,128)(2,1)S(1)} %get-tuple-element.93) | copy-start | bytes 2064388
  302.7 175.5 %reduce-scatter.4.cloned.1.call-start = ((), (), s32[]{:S(2)}) async-start(), calls=%async_computation.3 | async-start | bytes 3440640
  329.7 2.6 copy-start.2
  336.9 3.6 copy-start.14
  340.5 3.3 copy-start.41
  340.5 3.3 copy-start.42
  343.8 9.8 %copy-start.34 = (bf16[1,1280,256]{1,2,0:T(8,128)(2,1)S(1)}, bf16[1,1280,256]{1,2,0:T(8,128)(2,1)}, u32[]{:S(2)}) copy-start(bf16[1,1280,256]{1,2,0:T(8,128)(2,1)} %copy-done.33) | copy-start | bytes 1966084
  362.9 20.6 %slice-start.2 = ((s8[5505024]{0:T(1024)(128)(4,1)}), s8[1310720]{0:T(1024)(128)(4,1)S(1)}, s32[]{:S(2)}) async-start(s8[5505024]{0:T(1024)(128)(4,1)} %bitcast.282), calls=%async_computation.6 | async-start | bytes 2621440
  364.5 9.4 %copy-start.39 = (f32[2,128,2,256]{3,1,2,0:T(8,128)S(1)}, f32[2,128,2,256]{3,1,2,0:T(8,128)}, u32[]{:S(2)}) copy-start(f32[2,128,2,256]{3,1,2,0:T(8,128)} %fusion.22) | copy-start | bytes 1572868
  365.5 19.6 %collective-permute-start.4 = (bf16[2,256,256]{1,2,0:T(8,128)(2,1)}, bf16[2,256,256]{1,2,0:T(8,128)(2,1)}, u32[]{:S(2)}, u32[]{:S(2)}) collective-permute-start(bf16[2,256,256]{1,2,0:T(8,128)(2,1)} %get-tuple-element.97), channel_id=1, source_target_pairs={{4,0},{8,4},{12,8},{16,12},{20,16},{24,20},{28,24},{5,1},{9,5},{13... | collective-permute-start | bytes 786440 | tf_op jit(solution)/shard_map/ppermute | solution.py:44
  368.0 17.1 %collective-permute-start.5 = (bf16[2,256,256]{1,2,0:T(8,128)(2,1)}, bf16[2,256,256]{1,2,0:T(8,128)(2,1)}, u32[]{:S(2)}, u32[]{:S(2)}) collective-permute-start(bf16[2,256,256]{1,2,0:T(8,128)(2,1)} %get-tuple-element.100), channel_id=1, source_target_pairs={{8,0},{12,4},{16,8},{20,12},{24,16},{28,20},{9,1},{13,5},{17,9},{2... | collective-permute-start | bytes 786440 | tf_op jit(solution)/shard_map/ppermute | solution.py:44
  370.5 19.6 %collective-permute-start.6 = (bf16[2,256,256]{1,2,0:T(8,128)(2,1)}, bf16[2,256,256]{1,2,0:T(8,128)(2,1)}, u32[]{:S(2)}, u32[]{:S(2)}) collective-permute-start(bf16[2,256,256]{1,2,0:T(8,128)(2,1)} %get-tuple-element.99), channel_id=1, source_target_pairs={{12,0},{16,4},{20,8},{24,12},{28,16},{13,1},{17,5},{21,9},{25,13},... | collective-permute-start | bytes 786440 | tf_op jit(solution)/shard_map/ppermute | solution.py:44
  372.4 18.2 %collective-permute-start.7 = (bf16[2,256,256]{1,2,0:T(8,128)(2,1)}, bf16[2,256,256]{1,2,0:T(8,128)(2,1)}, u32[]{:S(2)}, u32[]{:S(2)}) collective-permute-start(bf16[2,256,256]{1,2,0:T(8,128)(2,1)} %get-tuple-element.98), channel_id=1, source_target_pairs={{16,0},{20,4},{24,8},{28,12},{17,1},{21,5},{25,9},{29,13},{18,2},{... | collective-permute-start | bytes 786440 | tf_op jit(solution)/shard_map/ppermute | solution.py:44
  376.6 3.6 copy-start.56
  378.6 4.8 slice-start.3
  383.5 7.2 %copy-start.20 = (f32[2,128,1280,1]{2,1,3,0:T(8,128)S(1)}, f32[2,128,1280,1]{2,1,3,0:T(8,128)}, u32[]{:S(2)}) copy-start(f32[2,128,1280,1]{2,1,3,0:T(8,128)} %fusion.21) | copy-start | bytes 3932164
  385.1 7.1 %copy-start.36 = (f32[256,64]{0,1:T(8,128)S(1)}, f32[256,64]{0,1:T(8,128)}, u32[]{:S(2)}) copy-start(f32[256,64]{0,1:T(8,128)} %copy-done.35) | copy-start | bytes 196612
  385.1 7.1 %copy-start.24 = (f32[256,256]{0,1:T(8,128)S(1)}, f32[256,256]{0,1:T(8,128)}, u32[]{:S(2)}) copy-start(f32[256,256]{0,1:T(8,128)} %copy-done.23) | copy-start | bytes 786436
  385.1 7.1 %copy-start.61 = (f32[128]{0:T(128)S(1)}, f32[128]{0:T(128)}, u32[]{:S(2)}) copy-start(f32[128]{0:T(128)} %param.25) | copy-start | bytes 1540
  397.2 2.8 copy-start.12
  397.2 2.8 copy-start.37
  399.9 12.3 %copy-start.4 = (bf16[256,1344]{1,0:T(8,128)(2,1)S(1)}, bf16[256,1344]{1,0:T(8,128)(2,1)}, u32[]{:S(2)}) copy-start(bf16[256,1344]{1,0:T(8,128)(2,1)} %copy-done.3) | copy-start | bytes 2064388
  399.9 12.3 %copy-start.51 = (f32[256]{0:T(256)S(1)}, f32[256]{0:T(256)}, u32[]{:S(2)}) copy-start(f32[256]{0:T(256)} %copy-done.50) | copy-start | bytes 3076
  480.5 9.9 %copy-start.58 = (f32[256]{0:T(256)S(1)}, f32[256]{0:T(256)}, u32[]{:S(2)}) copy-start(f32[256]{0:T(256)} %get-tuple-element.129) | copy-start | bytes 3076
  480.5 10.5 %copy-start.6 = (bf16[256,1344]{1,0:T(8,128)(2,1)S(1)}, bf16[256,1344]{1,0:T(8,128)(2,1)}, u32[]{:S(2)}) copy-start(bf16[256,1344]{1,0:T(8,128)(2,1)} %copy-done.5) | copy-start | bytes 2064388
  480.5 10.5 %copy-start.57 = (f32[256]{0:T(256)S(1)}, f32[256]{0:T(256)}, u32[]{:S(2)}) copy-start(f32[256]{0:T(256)} %get-tuple-element.130) | copy-start | bytes 3076
  490.9 4.4 copy-start.1
  (36 other events, 54.0 us)
Sparse Core Ops, SparseCore 0:
  9.6 27.3 all-gather.2
  302.8 26.8 all-gather.4
  397.3 47.1 reduce-scatter.3
